TPU v7x, 128 devices: a whole 4x4x4 slice. The times are simulated.
128 devices in a mesh: lev: 4 (over z_hi, core), win: 32 (over x, z_lo, y).
Axes of the slice: x: 4, y: 4, z: 4 (z_hi: 2, z_lo: 2; z = z_hi * 2 + z_lo), core: 2. Of those that a mesh axis runs over, the one named last changes fastest.
Arguments:
- fields: bfloat16 [12, 36864, 512], P('lev', 'win'), may hold values from -6 to 6
- patch_order: int32 [36864], replicated, may hold values from 0 to 36863, as said below
- shift_offsets: int32 [2], replicated, may hold values from 1 to 11
- latent_query: bfloat16 [3, 512], replicated, may hold values from -72 to 72
- enc_kv: bfloat16 [512, 1024], replicated, may hold values from -0.25 to 0.25
- enc_out: bfloat16 [512, 512], replicated, may hold values from -0.25 to 0.25
- qkv_a: bfloat16 [512, 1536], replicated, may hold values from -1 to 10
- proj_a: bfloat16 [512, 512], replicated, may hold values from -0.25 to 0.25
- merge_w: bfloat16 [2048, 1024], replicated, may hold values from -0.125 to 0.125
- qkv_b: bfloat16 [1024, 3072], replicated, may hold values from -1 to 10
- proj_b: bfloat16 [1024, 1024], replicated, may hold values from -0.1875 to 0.1875
- expand_w: bfloat16 [1024, 2048], replicated, may hold values from -0.1875 to 0.1875
- qkv_c: bfloat16 [512, 1536], replicated, may hold values from -1 to 10
- proj_c: bfloat16 [512, 512], replicated, may hold values from -0.25 to 0.25
Outputs:
- result: bfloat16 [48, 768, 3, 512], P('lev', 'win')
Inputs may be any that keep to these rules, and one draw needn't show every extreme that they name: `patch_order`: A permutation of the 36864 grid patches over the stored slots; the 1152 slots of each index of win hold exactly 9 patches of every pair of latitude band (12 rows) and longitude shard (24 columns), in no particular order.
All inputs are finite; a program needn't handle non-finite values.
Results may differ from a plain program's by a relative error of at most 0.015.
Values may be sent and summed in bfloat16 or wider, within the bound.
A program may use at most 256 MiB of HBM per device.

v0:
```python
import functools
import math

import jax
import jax.numpy as jnp
import numpy as np
from jax import lax
from jax.experimental import pallas as pl
from jax.experimental.pallas import tpu as pltpu
from jax.sharding import PartitionSpec as P

D = 512
HEADS = 16
LATENT = 3
PLAT = 12
PLON = 24
N_LEV = 4
N_WIN = 32
PSH = 1152
PER = 9
MSG = 32
CHUNK = 144
epsilon = 1e-05
BF = jnp.bfloat16
F32 = jnp.float32
MESH = pl.DeviceIdType.MESH
FAR = -1.0e6
VMEM = pl.BlockSpec(memory_space=pltpu.VMEM)
SMEM = pl.BlockSpec(memory_space=pltpu.SMEM)
ANY = pl.BlockSpec(memory_space=pl.ANY)


def params(mib=60, **more):
    return pltpu.CompilerParams(vmem_limit_bytes=mib << 20, **more)


def dot(a, b):
    return jnp.dot(a, b, preferred_element_type=F32)


def dot_nt(a, b):
    return lax.dot_general(a, b, (((1,), (1,)), ((), ())), preferred_element_type=F32)


def iota(shape, axis):
    return lax.broadcasted_iota(jnp.int32, shape, axis).astype(F32)


def div(values, by):
    return jnp.floor((values + 0.5) * (1.0 / by))


def hot(condition):
    return jnp.where(condition, 1.0, 0.0).astype(BF)


def group_ids(first_column):
    ids = np.full((4, 56), FAR, np.float32)
    for sub in range(4):
        for q in range(54):
            column = first_column + 2 * (q // 18) + (sub & 1)
            ids[sub, q] = column * 36 + (2 * (q % 6) + (sub >> 1)) * 3 + q % 18 // 6
    return ids


def half_ids(band, first_column):
    ids = np.full((112,), 2 * FAR, np.float32)
    for q in range(108):
        ids[q] = (first_column + q // 18) * 36 + (band * 6 + q % 6) * 3 + q % 18 // 6
    return ids


def tables():
    spread = np.concatenate([group_ids(6 * g).reshape(-1) for g in range(-1, 5)])
    windows = np.concatenate(
        [np.concatenate([half_ids(b, 0), half_ids(b, 6)]) for _ in range(2) for b in range(2)]
    )
    held = np.zeros((8, 1344), np.float32)
    held[0] = np.concatenate(
        [windows]
        + [half_ids(b, 6 - PLON) for b in range(2)]
        + [half_ids(b, PLON) for b in range(2)]
    )
    held[1, :448] = 1.0
    by_sub = np.stack([group_ids(6 * g) for g in range(4)], axis=1).reshape(-1)
    final = np.zeros((PLAT, LATENT, PLON), np.float32)
    for r in range(PLAT):
        for a in range(LATENT):
            for c in range(PLON):
                final[r, a, c] = c * 36 + r * 3 + a
    return (
        jnp.asarray(spread[None]),
        jnp.asarray(windows[:, None]),
        jnp.asarray(held),
        jnp.asarray(by_sub[:, None]),
        jnp.asarray(final.reshape(-1, 1)),
    )


def sort_kernel(core_ref, slots_ref, x_ref, keep_ref, send_ref, meta_ref, perm):
    @pl.when(pl.program_id(0) == 0)
    def _():
        core = core_ref[0].astype(F32)
        p = slots_ref[...].astype(F32)
        row = div(p, 768.0)
        column = p - row * 768.0
        band = div(row, 12.0)
        shard = div(column, 24.0)
        row = row - band * 12.0
        column = column - shard * 24.0
        half = div(band, 2.0)
        other = jnp.abs(band - 2.0 * half - core)
        key = other * 64.0 + half * 32.0 + shard
        member = hot(iota((128, PSH), 0) == key)
        upper = hot(iota((128, 128), 0) < iota((128, 128), 1))
        seen = jnp.zeros((128, 1), F32)
        ranks = []
        for b in range(PSH // 128):
            piece = member[:, b * 128 : (b + 1) * 128]
            wide = piece.astype(F32)
            ranks.append(jnp.sum(wide * (dot(piece, upper) + seen), axis=0, keepdims=True))
            seen = seen + jnp.sum(wide, axis=1, keepdims=True)
        target = key * PER + jnp.concatenate(ranks, axis=1)
        for b in range(PSH // 128):
            perm[b * 128 : (b + 1) * 128, :] = hot(iota((128, PSH), 0) + b * 128.0 == target)
        j = div(column, 2.0)
        group = div(j, 3.0)
        i = div(row, 2.0)
        sub = 2.0 * (row - 2.0 * i) + column - 2.0 * j
        base = group * 224.0 + sub * 56.0 + (j - 3.0 * group) * 18.0 + i
        high = div(base, 16.0)
        low = base - 16.0 * high
        at = iota((128, PSH), 0)
        meta = jnp.where(at == 48.0, high, jnp.where(at == 49.0, low, 0.0)).astype(BF)
        meta_ref[...] = dot_nt(perm[0:576, :], meta).astype(BF)

    done = dot(perm[...], x_ref[0])
    keep_ref[0] = done[:576].astype(BF)
    send_ref[0] = done[576:].astype(BF)


def sort_fields(core, slots, fields):
    levels = fields.shape[0]
    return pl.pallas_call(
        sort_kernel,
        grid=(levels,),
        in_specs=[
            SMEM,
            pl.BlockSpec((1, PSH), lambda l: (0, 0)),
            pl.BlockSpec((1, PSH, D), lambda l: (l, 0, 0)),
        ],
        out_specs=[
            pl.BlockSpec((1, 576, D), lambda l: (l, 0, 0)),
            pl.BlockSpec((1, 576, D), lambda l: (l, 0, 0)),
            pl.BlockSpec((576, 128), lambda l: (0, 0)),
        ],
        out_shape=[
            jax.ShapeDtypeStruct((levels, 576, D), BF),
            jax.ShapeDtypeStruct((levels, 576, D), BF),
            jax.ShapeDtypeStruct((576, 128), BF),
        ],
        scratch_shapes=[pltpu.VMEM((PSH, PSH), BF)],
        compiler_params=params(),
        name="sort_fields",
    )(core, slots, fields)


def encode_kernel(own_ref, got_ref, meta_ref, kv_ref, query_ref, out_ref, score_w, spread_w, stat_w, pick, stack):
    @pl.when(pl.program_id(0) == 0)
    def _():
        c = iota((128, D), 0)
        lane = iota((128, D), 1)
        a = div(c, 16.0)
        q = query_ref[...].astype(F32)
        chosen = jnp.where(a == 0.0, q[0:1], jnp.where(a == 1.0, q[1:2], q[2:3]))
        mine = (c - 16.0 * a == div(lane, 32.0)) & (c < 48.0)
        heads = jnp.where(mine, chosen, 0.0).astype(BF)
        folded = dot_nt(kv_ref[:, :D], heads) * (1.0 / math.sqrt(D // HEADS))
        high = folded.astype(BF)
        score_w[:, 0:128] = high
        score_w[:, 128:256] = (folded - high.astype(F32)).astype(BF)
        for a in range(LATENT):
            spread_w[:, a * D : (a + 1) * D] = hot(c == 16.0 * a + div(lane, 32.0))
            s = iota((128, 128), 0)
            t = iota((128, 128), 1)
            t = t - 64.0 * div(t, 64.0)
            for piece in range(3):
                here = (t >= 16.0 * piece) & (t < 16.0 * piece + 16.0)
                stat_w[piece * 128 : (piece + 1) * 128, a * 128 : (a + 1) * 128] = hot(
                    here & (s == 16.0 * a + t - 16.0 * piece)
                )
            stat_w[384:512, a * 128 : (a + 1) * 128] = hot((t >= 48.0) & (t < 50.0) & (s == t))
        lane = iota((1, 6 * CHUNK), 1)
        kind = div(lane, float(CHUNK))
        slot = lane - kind * CHUNK
        stats = kind >= 3.0
        a = jnp.where(stats, kind - 3.0, kind)
        dest = div(slot, float(PER))
        k = a * PER + slot - dest * PER
        row = dest * MSG + jnp.where(stats, 27.0 + div(k, 8.0), k)
        for b in range(4):
            pick[b * 128 : (b + 1) * 128, :] = hot(iota((128, 6 * CHUNK), 0) + b * 128.0 == row)

    xs = [own_ref[l] for l in range(3)] + [got_ref[l] for l in range(3)]
    scores = []
    for x in xs:
        both = dot(x, score_w[...])
        scores.append(both[:, :128] + both[:, 128:])
    peak = functools.reduce(jnp.maximum, scores)
    weights = [jnp.exp(s - peak) for s in scores]
    total = functools.reduce(jnp.add, weights)
    mixes = [jnp.zeros((CHUNK, D), F32)] * LATENT
    for x, w in zip(xs, weights):
        value = dot(x, kv_ref[:, D:]).astype(BF).astype(F32)
        wide = dot((w / total).astype(BF), spread_w[...])
        mixes = [m + wide[:, a * D : (a + 1) * D] * value for a, m in enumerate(mixes)]
    logsum = peak + jnp.log(total)
    high = logsum.astype(BF)
    rest = logsum - high.astype(F32)
    middle = rest.astype(BF)
    low = (rest - middle.astype(F32)).astype(BF)
    stats = dot(jnp.concatenate([high, middle, low, meta_ref[...]], axis=1), stat_w[...])
    slot = iota((CHUNK, D), 0)
    rank = slot - PER * div(slot, float(PER))
    block = div(iota((CHUNK, D), 1), 64.0)
    for a in range(LATENT):
        stack[a * CHUNK : (a + 1) * CHUNK, :] = mixes[a].astype(BF)
        k = rank + PER * a
        tiled = jnp.concatenate([stats[:, a * 128 : (a + 1) * 128]] * 4, axis=1)
        stack[(3 + a) * CHUNK : (4 + a) * CHUNK, :] = jnp.where(
            block == k - 8.0 * div(k, 8.0), tiled, 0.0
        ).astype(BF)
    out_ref[...] = dot(pick[...], stack[...]).astype(BF)


def encode(own, got, meta, enc_kv, latent_query):
    return pl.pallas_call(
        encode_kernel,
        grid=(576 // CHUNK,),
        in_specs=[
            pl.BlockSpec((3, CHUNK, D), lambda i: (0, i, 0)),
            pl.BlockSpec((3, CHUNK, D), lambda i: (0, i, 0)),
            pl.BlockSpec((CHUNK, 128), lambda i: (i, 0)),
            VMEM,
            VMEM,
        ],
        out_specs=pl.BlockSpec((16 * MSG, D), lambda i: (i, 0)),
        out_shape=jax.ShapeDtypeStruct((64 * MSG, D), BF),
        scratch_shapes=[
            pltpu.VMEM((D, 256), BF),
            pltpu.VMEM((128, LATENT * D), BF),
            pltpu.VMEM((512, LATENT * 128), BF),
            pltpu.VMEM((16 * MSG, 6 * CHUNK), BF),
            pltpu.VMEM((6 * CHUNK, D), BF),
        ],
        compiler_params=params(),
        name="encode",
    )(own, got, meta, enc_kv, latent_query)


def swap_kernel(msg_ref, out_ref, send_sem, recv_sem, own_sem):
    lev = lax.axis_index("lev")
    win = lax.axis_index("win")
    core = lax.rem(lev, 2)
    me = (lev // 2) * N_WIN + win
    count = 2 * N_WIN

    def device(index):
        return ((index // N_WIN) * 2 + core, lax.rem(index, N_WIN))

    own = pltpu.make_async_copy(msg_ref.at[me], out_ref.at[me], own_sem)
    own.start()
    barrier = pltpu.get_barrier_semaphore()

    @pl.loop(1, count)
    def _(k):
        pl.semaphore_signal(
            barrier, inc=1, device_id=device(lax.rem(me + k, count)), device_id_type=MESH
        )

    pl.semaphore_wait(barrier, count - 1)

    def copy(k):
        dest = lax.rem(me + k, count)
        return pltpu.make_async_remote_copy(
            src_ref=msg_ref.at[dest],
            dst_ref=out_ref.at[me],
            send_sem=send_sem.at[k],
            recv_sem=recv_sem.at[k],
            device_id=device(dest),
            device_id_type=MESH,
        )

    @pl.loop(1, count)
    def _(k):
        copy(k).start()

    @pl.loop(1, count)
    def _(k):
        copy(k).wait()

    own.wait()


def swap(messages):
    return pl.pallas_call(
        swap_kernel,
        out_shape=jax.ShapeDtypeStruct((64, MSG, D), BF),
        in_specs=[ANY],
        out_specs=ANY,
        scratch_shapes=[
            pltpu.SemaphoreType.DMA((64,)),
            pltpu.SemaphoreType.DMA((64,)),
            pltpu.SemaphoreType.DMA,
        ],
        compiler_params=pltpu.CompilerParams(collective_id=0, has_side_effects=True),
        name="swap",
    )(messages)


def settle_kernel(got_ref, query_ref, out_w_ref, grid_ref, latents, rows):
    m = iota((256, 256), 0)
    k = m - MSG * div(m, float(MSG))
    pick = hot((k < 27.0) & (iota((256, 256), 1) == m - k + 27.0 + div(k, 8.0)))
    k = iota((256, D), 0)
    k = k - MSG * div(k, float(MSG))
    mask = div(iota((256, D), 1), 64.0) == k - 8.0 * div(k, 8.0)
    lane = iota((D, D), 0)
    lane = lane - 64.0 * div(lane, 64.0)
    fold = hot((lane < 48.0) & (lane - 16.0 * div(lane, 16.0) == div(iota((D, D), 1), 32.0)))
    lane = iota((D, 128), 0)
    lane = lane - 64.0 * div(lane, 64.0)
    base_w = jnp.where(lane == 48.0, 16.0, jnp.where(lane == 49.0, 1.0, 0.0)).astype(BF)
    q = query_ref[...].astype(F32)
    bias = jnp.where(k < 9.0, q[0:1], jnp.where(k < 18.0, q[1:2], q[2:3]))
    k = iota((256, 128), 0)
    k = k - MSG * div(k, float(MSG))
    for c in range(4):
        values = [got_ref[g, c * 256 : (c + 1) * 256, :] for g in range(2)]
        stats = [jnp.where(mask, dot(pick, v), 0.0).astype(BF) for v in values]
        logs = [dot(s, fold) for s in stats]
        peak = jnp.maximum(logs[0], logs[1])
        weights = [jnp.exp(l - peak) for l in logs]
        mixed = weights[0] * values[0].astype(F32) + weights[1] * values[1].astype(F32)
        encoded = (mixed / (weights[0] + weights[1])).astype(BF)
        latents[c * 256 : (c + 1) * 256, :] = (dot(encoded, out_w_ref[...]) + bias).astype(BF)
        place = dot(stats[0], base_w) + 6.0 * div(k, 9.0)
        place = jnp.where(k < 27.0, place, FAR)
        rows[:, c * 256 : (c + 1) * 256] = jnp.transpose(place)[0:8, :]
    where = rows[0:1, :]
    for b in range(4):
        chosen = hot(iota((224, 1024), 0) + 224.0 * b == where)
        grid_ref[b] = dot(chosen, latents[...]).astype(BF)


def settle(got, latent_query, enc_out):
    return pl.pallas_call(
        settle_kernel,
        in_specs=[VMEM] * 3,
        out_specs=VMEM,
        out_shape=jax.ShapeDtypeStruct((4, 224, D), BF),
        scratch_shapes=[pltpu.VMEM((1024, D), BF), pltpu.VMEM((8, 1024), F32)],
        compiler_params=params(),
        name="settle",
    )(got, latent_query, enc_out)


def normalize(values):
    offsets = values - jnp.mean(values, axis=-1, keepdims=True)
    spread = jnp.mean(offsets * offsets, axis=-1, keepdims=True)
    return offsets * lax.rsqrt(spread + epsilon)


def heads_of_group(qkv, out, rows, g, width, bias):
    column = pl.multiple_of(g * 128, 128)
    q = qkv[rows, pl.ds(column, 128)]
    k = qkv[rows, pl.ds(width + column, 128)]
    v = qkv[rows, pl.ds(2 * width + column, 128)]
    v = jnp.concatenate([v, jnp.ones_like(v)], axis=1)
    head = div(iota((1, 128), 1), 32.0)
    scale = math.log2(math.e) / math.sqrt(32.0)
    total = jnp.zeros((224, 128), F32)
    for h in range(4):
        only = head == float(h)
        scores = dot_nt(q * hot(only), k) + bias
        peak = jnp.max(scores, axis=1, keepdims=True)
        weights = jnp.exp2((scores - peak) * scale).astype(BF)
        mixed = dot(weights, v)
        total = total + jnp.where(only, mixed[:, :128] / mixed[:, 128:], 0.0)
    out[rows, pl.ds(column, 128)] = total.astype(BF)


def key_bias(slots, valid):
    lane = iota((1, 224), 1)
    lane = lane - slots * div(lane, float(slots))
    return jnp.where(lane < valid, 0.0, -1.0e30)


def shift_starts(shift_ref):
    s = shift_ref[0]
    near = s.astype(F32)
    far = jnp.where(s <= 6, s + 12, s - 12).astype(F32)
    return near, far


def window_kernel(
    shift_ref, before_ref, own_ref, after_ref, spread_ref, windows_ref, w_ref, proj_ref, out_ref, cells, x, qkv, mixed
):
    near, far = shift_starts(shift_ref)
    cells[0:224, :] = before_ref[...]
    for g in range(4):
        cells[(g + 1) * 224 : (g + 2) * 224, :] = own_ref[g]
    cells[1120:1344, :] = after_ref[...]
    for n in range(4):
        rows = slice(n * 224, (n + 1) * 224)
        target = windows_ref[rows, :] + 36.0 * (near if n < 2 else far)
        x[rows, :] = dot(hot(target == spread_ref[...]), cells[...]).astype(BF)
    for n in range(4):
        rows = slice(n * 224, (n + 1) * 224)
        normed = normalize(x[rows, :].astype(F32)).astype(BF)
        qkv[rows, :] = dot(normed, w_ref[...]).astype(BF)
    bias = key_bias(112, 108)

    @pl.loop(0, 16)
    def _(step):
        rows = pl.ds(pl.multiple_of((step // 4) * 224, 224), 224)
        heads_of_group(qkv, mixed, rows, lax.rem(step, 4), D, bias)

    for n in range(4):
        rows = slice(n * 224, (n + 1) * 224)
        out_ref[n] = (x[rows, :].astype(F32) + dot(mixed[rows, :], proj_ref[...])).astype(BF)


def window_block(shift, before, own, after, spread, windows, w_qkv, w_proj):
    return pl.pallas_call(
        window_kernel,
        in_specs=[SMEM] + [VMEM] * 7,
        out_specs=VMEM,
        out_shape=jax.ShapeDtypeStruct((4, 224, D), BF),
        scratch_shapes=[
            pltpu.VMEM((1344, D), BF),
            pltpu.VMEM((896, D), BF),
            pltpu.VMEM((896, 3 * D), BF),
            pltpu.VMEM((896, D), BF),
        ],
        compiler_params=params(),
        name="window_block",
    )(shift, before, own, after, spread, windows, w_qkv, w_proj)


def held_ids(shift_ref, held_ref):
    near, far = shift_starts(shift_ref)
    local = held_ref[1:2, :]
    return held_ref[0:1, :] + 36.0 * jnp.where(local > 0.5, near, far)


def gather_cells(cells, own_ref, before_ref, after_ref):
    for n in range(4):
        cells[n * 224 : (n + 1) * 224, :] = own_ref[n]
    for b in range(2):
        cells[896 + b * 112 : 1008 + b * 112, :] = before_ref[b]
        cells[1120 + b * 112 : 1232 + b * 112, :] = after_ref[b]


def coarse_kernel(
    shift_ref,
    own_ref,
    before_ref,
    after_ref,
    held_ref,
    sub_ref,
    merge_ref,
    w_ref,
    proj_ref,
    expand_ref,
    out_ref,
    cells,
    first,
    qkv,
    mixed,
):
    gather_cells(cells, own_ref, before_ref, after_ref)
    ids = held_ids(shift_ref, held_ref)
    total = jnp.zeros((224, 1), F32)
    for sub in range(4):
        rows = slice(sub * 224, (sub + 1) * 224)
        piece = dot(hot(sub_ref[rows, :] == ids), cells[...])
        first[rows, :] = piece.astype(BF)
        total = total + jnp.sum(piece, axis=1, keepdims=True)
    centre = total * (1.0 / (4 * D))
    spread = jnp.zeros((224, 1), F32)
    for sub in range(4):
        offsets = first[sub * 224 : (sub + 1) * 224, :].astype(F32) - centre
        spread = spread + jnp.sum(offsets * offsets, axis=1, keepdims=True)
    scale = lax.rsqrt(spread * (1.0 / (4 * D)) + epsilon)
    down = jnp.zeros((224, 2 * D), F32)
    for sub in range(4):
        offsets = first[sub * 224 : (sub + 1) * 224, :].astype(F32) - centre
        down = down + dot((offsets * scale).astype(BF), merge_ref[sub * D : (sub + 1) * D, :])
    down = down.astype(BF).astype(F32)
    qkv[...] = dot(normalize(down).astype(BF), w_ref[...]).astype(BF)
    bias = key_bias(56, 54)

    @pl.loop(0, 8)
    def _(g):
        heads_of_group(qkv, mixed, pl.ds(0, 224), g, 2 * D, bias)

    coarse = (down + dot(mixed[...], proj_ref[...])).astype(BF).astype(F32)
    normed = normalize(coarse).astype(BF)
    for sub in range(4):
        grown = dot(normed, expand_ref[:, sub * D : (sub + 1) * D])
        joined = grown + first[sub * 224 : (sub + 1) * 224, :].astype(F32)
        for g in range(4):
            out_ref[g, sub] = joined[g * 56 : (g + 1) * 56, :].astype(BF)


def coarse_block(shift, own, before, after, held, by_sub, merge_w, w_qkv, w_proj, expand_w):
    return pl.pallas_call(
        coarse_kernel,
        in_specs=[SMEM] + [VMEM] * 9,
        out_specs=VMEM,
        out_shape=jax.ShapeDtypeStruct((4, 4, 56, D), BF),
        scratch_shapes=[
            pltpu.VMEM((1344, D), BF),
            pltpu.VMEM((896, D), BF),
            pltpu.VMEM((224, 6 * D), BF),
            pltpu.VMEM((224, 2 * D), BF),
        ],
        compiler_params=params(),
        name="coarse_block",
    )(shift, own, before, after, held, by_sub, merge_w, w_qkv, w_proj, expand_w)


def final_kernel(shift_ref, own_ref, before_ref, after_ref, held_ref, final_ref, out_ref, cells):
    gather_cells(cells, own_ref, before_ref, after_ref)
    ids = held_ids(shift_ref, held_ref)
    for b in range(4):
        rows = slice(b * 216, (b + 1) * 216)
        out_ref[rows, :] = dot(hot(final_ref[rows, :] == ids), cells[...]).astype(BF)


def final_order(shift, own, before, after, held, final):
    return pl.pallas_call(
        final_kernel,
        in_specs=[SMEM] + [VMEM] * 5,
        out_specs=VMEM,
        out_shape=jax.ShapeDtypeStruct((PLAT * LATENT * PLON, D), BF),
        scratch_shapes=[pltpu.VMEM((1344, D), BF)],
        compiler_params=params(),
        name="final_order",
    )(shift, own, before, after, held, final)


def passed_along(value, axis, steps):
    count = lax.axis_size(axis)
    pairs = [(source, (source + steps) % count) for source in range(count)]
    return lax.ppermute(value, axis, pairs)


def from_sides(to_previous, to_next):
    return passed_along(to_next, "win", 1), passed_along(to_previous, "win", -1)


def local(
    fields,
    patch_order,
    shift_offsets,
    latent_query,
    enc_kv,
    enc_out,
    qkv_a,
    proj_a,
    merge_w,
    qkv_b,
    proj_b,
    expand_w,
    qkv_c,
    proj_c,
):
    lev_at = lax.axis_index("lev")
    win_at = lax.axis_index("win")
    spread, windows, held, by_sub, final = tables()
    slots = lax.dynamic_slice_in_dim(patch_order, win_at * PSH, PSH, 0).reshape(1, PSH)
    core = lax.rem(lev_at, 2).astype(jnp.int32).reshape(1)
    keep, send, meta = sort_fields(core, slots, fields)
    got = lax.ppermute(send, "lev", [(0, 1), (1, 0), (2, 3), (3, 2)])
    messages = encode(keep, got, meta, enc_kv, latent_query)
    arrived = swap(messages.reshape(64, MSG, D)).reshape(2, 32 * MSG, D)
    grid = settle(arrived, latent_query, enc_out)

    def shifted(grid, shift, w_qkv, w_proj):
        before, after = from_sides(grid[0], grid[3])
        done = window_block(shift, before, grid, after, spread, windows, w_qkv, w_proj)
        return (done,) + from_sides(done[2:, :112], done[2:, 112:])

    shift = shift_offsets[0:1]
    done, before, after = shifted(grid, shift, qkv_a, proj_a)
    joined = coarse_block(
        shift, done, before, after, held, by_sub, merge_w, qkv_b, proj_b, expand_w
    ).reshape(4, 224, D)
    shift = shift_offsets[1:2]
    done, before, after = shifted(joined, shift, qkv_c, proj_c)
    result = final_order(shift, done, before, after, held, final)
    return result.reshape(PLAT, LATENT, PLON, D).transpose(0, 2, 1, 3)


def solution(mesh):
    placed = (P("lev", "win", None),) + (P(),) * 13
    return jax.shard_map(
        local, mesh=mesh, in_specs=placed, out_specs=P("lev", "win", None, None), check_vma=False
    )
```

profile of v0, /device:TPU:0, one launch (start us, length us, event | category | flops | bytes accessed | tf_op | source)
XLA Modules:
  0.0 197.7 jit_solution(9854632885376625606)
XLA Ops:
  0.0 0.8 dynamic_slice.3
  1.4 8.8 %sort_fields.1 = (bf16[3,576,512]{2,1,0:T(8,128)(2,1)}, bf16[3,576,512]{2,1,0:T(8,128)(2,1)}, bf16[576,128]{1,0:T(8,128)(2,1)}) custom-call(s32[1]{0:T(128)} %bitcast.core_ref, s32[1,1152]{1,0:T(1,128)} %reshape.23.slots_ref, bf16[3,1152,512]{2,1,0:T(8,128)(2,1)} %x_ref.1), custom_call_target="tpu_custom_call" | custom-call | tf_op jit(solution)/shard_map/sort_fields/pallas_call | solution.py:144
  10.1 3.9 %collective-permute-done.got_ref = bf16[3,576,512]{2,1,0:T(8,128)(2,1)S(1)} collective-permute-done((bf16[3,576,512]{2,1,0:T(8,128)(2,1)}, bf16[3,576,512]{2,1,0:T(8,128)(2,1)S(1)}, u32[]{:S(2)}, u32[]{:S(2)}) %collective-permute-start) | collective-permute-done | bytes 1769504 | tf_op jit(solution)/shard_map/ppermute | solution.py:586
  14.0 1.2 copy-done
  15.3 12.5 %encode.1 = bf16[2048,512]{1,0:T(8,128)(2,1)} custom-call(bf16[3,576,512]{2,1,0:T(8,128)(2,1)} %get-tuple-element.8.own_ref, bf16[3,576,512]{2,1,0:T(8,128)(2,1)} %copy-done, bf16[576,128]{1,0:T(8,128)(2,1)} %get-tuple-element.10.meta_ref, bf16[512,1024]{1,0:T(8,128)(2,1)} %kv_ref.1, bf16[3,512]{1,0:T(4,128)(2,1)} %query_ref.3), custom_call_target="tpu_custom_call" | custom-call | tf_op jit(solution)/shard_map/encode/pallas_call | solution.py:237
  27.8 43.7 %swap.1 = bf16[64,32,512]{2,1,0:T(8,128)(2,1)} custom-call(bf16[64,32,512]{2,1,0:T(8,128)(2,1)} %bitcast.13), custom_call_target="tpu_custom_call" | custom-call | tf_op jit(solution)/shard_map/swap/pallas_call | solution.py:306
  71.5 7.7 %settle.1.own_ref = bf16[4,224,512]{2,1,0:T(8,128)(2,1)} custom-call(bf16[2,1024,512]{2,1,0:T(8,128)(2,1)} %bitcast.14, bf16[3,512]{1,0:T(4,128)(2,1)} %query_ref.3, bf16[512,512]{1,0:T(8,128)(2,1)} %out_w_ref.1), custom_call_target="tpu_custom_call" | custom-call | tf_op jit(solution)/shard_map/settle/pallas_call | solution.py:357
  79.2 1.1 slice_bitcast_fusion
  80.7 6.2 %collective-permute-start.2 = (bf16[224,512]{1,0:T(8,128)(2,1)S(1)}, bf16[224,512]{1,0:T(8,128)(2,1)S(1)}, u32[]{:S(2)}, u32[]{:S(2)}) collective-permute-start(bf16[224,512]{1,0:T(8,128)(2,1)S(1)} %get-tuple-element.17), channel_id=1, source_target_pairs={{0,31},{1,0},{2,1},{3,2},{4,3},{5,4},{6,5},{7,6},{8,7},{9,8},{10,9... | collective-permute-start | bytes 688136 | tf_op jit(solution)/shard_map/ppermute | solution.py:557
  87.5 3.9 %collective-permute-done.1.before_ref = bf16[224,512]{1,0:T(8,128)(2,1)S(1)} collective-permute-done((bf16[224,512]{1,0:T(8,128)(2,1)S(1)}, bf16[224,512]{1,0:T(8,128)(2,1)S(1)}, u32[]{:S(2)}, u32[]{:S(2)}) %collective-permute-start.1) | collective-permute-done | bytes 229408 | tf_op jit(solution)/shard_map/ppermute | solution.py:557
  92.1 20.9 %window_block.2.own_ref = bf16[4,224,512]{2,1,0:T(8,128)(2,1)} custom-call(s32[1]{0:T(128)} %get-tuple-element.19.shift_ref, bf16[224,512]{1,0:T(8,128)(2,1)} %copy-done.5, bf16[4,224,512]{2,1,0:T(8,128)(2,1)} %settle.1.own_ref, bf16[224,512]{1,0:T(8,128)(2,1)} %copy-done.7, f32[1,1344]{1,0:T(1,128)} %constant.29.clone.spread_ref, ...), custom_call_target="tpu_custom_call" | custom-call | tf_op jit(solution)/shard_map/window_block/pallas_call | solution.py:435
  113.0 1.1 fusion.2
  114.1 6.2 %collective-permute-start.4 = (bf16[2,112,512]{2,1,0:T(8,128)(2,1)S(1)}, bf16[2,112,512]{2,1,0:T(8,128)(2,1)S(1)}, u32[]{:S(2)}, u32[]{:S(2)}) collective-permute-start(bf16[2,112,512]{2,1,0:T(8,128)(2,1)S(1)} %get-tuple-element.15), channel_id=1, source_target_pairs={{0,31},{1,0},{2,1},{3,2},{4,3},{5,4},{6,5},{7,6},{8,7},{9,8},{10,9... | collective-permute-start | bytes 688136 | tf_op jit(solution)/shard_map/ppermute | solution.py:557
  120.4 4.0 %collective-permute-done.3.before_ref = bf16[2,112,512]{2,1,0:T(8,128)(2,1)S(1)} collective-permute-done((bf16[2,112,512]{2,1,0:T(8,128)(2,1)S(1)}, bf16[2,112,512]{2,1,0:T(8,128)(2,1)S(1)}, u32[]{:S(2)}, u32[]{:S(2)}) %collective-permute-start.3) | collective-permute-done | bytes 229408 | tf_op jit(solution)/shard_map/ppermute | solution.py:557
  125.1 0.7 copy-done.2
  125.8 21.5 %coarse_block.1 = bf16[4,4,56,512]{3,2,1,0:T(8,128)(2,1)} custom-call(s32[1]{0:T(128)} %get-tuple-element.19.shift_ref, bf16[4,224,512]{2,1,0:T(8,128)(2,1)} %window_block.2.own_ref, bf16[2,112,512]{2,1,0:T(8,128)(2,1)} %copy-done.1, bf16[2,112,512]{2,1,0:T(8,128)(2,1)} %copy-done.2, f32[8,1344]{1,0:T(8,128)} %constant.31.clone.held_ref, ...), custom_call_target="tpu_custom_call" | custom-call | tf_op jit(solution)/shard_map/coarse_block/pallas_call | solution.py:518
  147.3 1.1 fusion.1
  148.4 6.2 %collective-permute-start.6 = (bf16[224,512]{1,0:T(8,128)(2,1)S(1)}, bf16[224,512]{1,0:T(8,128)(2,1)S(1)}, u32[]{:S(2)}, u32[]{:S(2)}) collective-permute-start(bf16[224,512]{1,0:T(8,128)(2,1)S(1)} %bitcast.16), channel_id=1, source_target_pairs={{0,31},{1,0},{2,1},{3,2},{4,3},{5,4},{6,5},{7,6},{8,7},{9,8},{10,9... | collective-permute-start | bytes 688136 | tf_op jit(solution)/shard_map/ppermute | solution.py:557
  154.7 4.0 %collective-permute-done.5.before_ref = bf16[224,512]{1,0:T(8,128)(2,1)S(1)} collective-permute-done((bf16[224,512]{1,0:T(8,128)(2,1)S(1)}, bf16[224,512]{1,0:T(8,128)(2,1)S(1)}, u32[]{:S(2)}, u32[]{:S(2)}) %collective-permute-start.5) | collective-permute-done | bytes 229408 | tf_op jit(solution)/shard_map/ppermute | solution.py:557
  159.4 20.9 %window_block.3.own_ref = bf16[4,224,512]{2,1,0:T(8,128)(2,1)} custom-call(s32[1]{0:T(128)} %get-tuple-element.20.shift_ref, bf16[224,512]{1,0:T(8,128)(2,1)} %copy-done.6, bf16[4,224,512]{2,1,0:T(8,128)(2,1)} %bitcast.15, bf16[224,512]{1,0:T(8,128)(2,1)} %copy-done.8, f32[1,1344]{1,0:T(1,128)} %constant.29.clone.spread_ref, ...), custom_call_target="tpu_custom_call" | custom-call | tf_op jit(solution)/shard_map/window_block/pallas_call | solution.py:435
  180.3 1.1 fusion
  181.5 6.2 %collective-permute-start.8 = (bf16[2,112,512]{2,1,0:T(8,128)(2,1)S(1)}, bf16[2,112,512]{2,1,0:T(8,128)(2,1)S(1)}, u32[]{:S(2)}, u32[]{:S(2)}) collective-permute-start(bf16[2,112,512]{2,1,0:T(8,128)(2,1)S(1)} %get-tuple-element.11), channel_id=1, source_target_pairs={{0,31},{1,0},{2,1},{3,2},{4,3},{5,4},{6,5},{7,6},{8,7},{9,8},{10,9... | collective-permute-start | bytes 688136 | tf_op jit(solution)/shard_map/ppermute | solution.py:557
  187.7 4.0 %collective-permute-done.7.before_ref = bf16[2,112,512]{2,1,0:T(8,128)(2,1)S(1)} collective-permute-done((bf16[2,112,512]{2,1,0:T(8,128)(2,1)S(1)}, bf16[2,112,512]{2,1,0:T(8,128)(2,1)S(1)}, u32[]{:S(2)}, u32[]{:S(2)}) %collective-permute-start.7) | collective-permute-done | bytes 229408 | tf_op jit(solution)/shard_map/ppermute | solution.py:557
  193.1 4.7 %final_order.1 = bf16[864,512]{1,0:T(8,128)(2,1)} custom-call(s32[1]{0:T(128)} %get-tuple-element.20.shift_ref, bf16[4,224,512]{2,1,0:T(8,128)(2,1)} %window_block.3.own_ref, bf16[2,112,512]{2,1,0:T(8,128)(2,1)} %copy-done.3, bf16[2,112,512]{2,1,0:T(8,128)(2,1)} %copy-done.4, f32[8,1344]{1,0:T(8,128)} %constant.31.clone.held_ref, ...), custom_call_target="tpu_custom_call" | custom-call | tf_op jit(solution)/shard_map/final_order/pallas_call | solution.py:543
  (29 shorter events, 5.4 us)
Async XLA Ops:
  10.1 3.9 %collective-permute-start = (bf16[3,576,512]{2,1,0:T(8,128)(2,1)}, bf16[3,576,512]{2,1,0:T(8,128)(2,1)S(1)}, u32[]{:S(2)}, u32[]{:S(2)}) collective-permute-start(bf16[3,576,512]{2,1,0:T(8,128)(2,1)} %get-tuple-element.9), channel_id=1, source_target_pairs={{0,32},{32,0},{64,96},{96,64},{1,33},{33,1},{65,97},{97,65},{2,34}... | collective-permute-start | bytes 5308424 | tf_op jit(solution)/shard_map/ppermute | solution.py:586
  14.0 1.2 copy-start
  71.5 15.3 %copy-start.9 = (s32[2]{0:T(128)S(1)}, s32[2]{0:T(128)}, u32[]{:S(2)}) copy-start(s32[2]{0:T(128)} %param.21) | copy-start | bytes 28
  80.3 11.0 %collective-permute-start.1 = (bf16[224,512]{1,0:T(8,128)(2,1)S(1)}, bf16[224,512]{1,0:T(8,128)(2,1)S(1)}, u32[]{:S(2)}, u32[]{:S(2)}) collective-permute-start(bf16[224,512]{1,0:T(8,128)(2,1)S(1)} %get-tuple-element.18), channel_id=1, source_target_pairs={{0,1},{1,2},{2,3},{3,4},{4,5},{5,6},{6,7},{7,8},{8,9},{9,10},{10,1... | collective-permute-start | bytes 688136 | tf_op jit(solution)/shard_map/ppermute | solution.py:557
  80.7 10.7 %collective-permute-start.2 = (bf16[224,512]{1,0:T(8,128)(2,1)S(1)}, bf16[224,512]{1,0:T(8,128)(2,1)S(1)}, u32[]{:S(2)}, u32[]{:S(2)}) collective-permute-start(bf16[224,512]{1,0:T(8,128)(2,1)S(1)} %get-tuple-element.17), channel_id=1, source_target_pairs={{0,31},{1,0},{2,1},{3,2},{4,3},{5,4},{6,5},{7,6},{8,7},{9,8},{10,9... | collective-permute-start | bytes 688136 | tf_op jit(solution)/shard_map/ppermute | solution.py:557
  91.3 0.7 copy-start.5
  91.4 0.8 copy-start.7
  114.1 10.3 %collective-permute-start.3 = (bf16[2,112,512]{2,1,0:T(8,128)(2,1)S(1)}, bf16[2,112,512]{2,1,0:T(8,128)(2,1)S(1)}, u32[]{:S(2)}, u32[]{:S(2)}) collective-permute-start(bf16[2,112,512]{2,1,0:T(8,128)(2,1)S(1)} %get-tuple-element.16), channel_id=1, source_target_pairs={{0,1},{1,2},{2,3},{3,4},{4,5},{5,6},{6,7},{7,8},{8,9},{9,10},{10,1... | collective-permute-start | bytes 688136 | tf_op jit(solution)/shard_map/ppermute | solution.py:557
  114.1 10.2 %collective-permute-start.4 = (bf16[2,112,512]{2,1,0:T(8,128)(2,1)S(1)}, bf16[2,112,512]{2,1,0:T(8,128)(2,1)S(1)}, u32[]{:S(2)}, u32[]{:S(2)}) collective-permute-start(bf16[2,112,512]{2,1,0:T(8,128)(2,1)S(1)} %get-tuple-element.15), channel_id=1, source_target_pairs={{0,31},{1,0},{2,1},{3,2},{4,3},{5,4},{6,5},{7,6},{8,7},{9,8},{10,9... | collective-permute-start | bytes 688136 | tf_op jit(solution)/shard_map/ppermute | solution.py:557
  124.4 0.7 copy-start.1
  125.1 0.7 copy-start.2
  148.4 10.3 %collective-permute-start.5 = (bf16[224,512]{1,0:T(8,128)(2,1)S(1)}, bf16[224,512]{1,0:T(8,128)(2,1)S(1)}, u32[]{:S(2)}, u32[]{:S(2)}) collective-permute-start(bf16[224,512]{1,0:T(8,128)(2,1)S(1)} %bitcast.17), channel_id=1, source_target_pairs={{0,1},{1,2},{2,3},{3,4},{4,5},{5,6},{6,7},{7,8},{8,9},{9,10},{10,1... | collective-permute-start | bytes 688136 | tf_op jit(solution)/shard_map/ppermute | solution.py:557
  148.4 10.2 %collective-permute-start.6 = (bf16[224,512]{1,0:T(8,128)(2,1)S(1)}, bf16[224,512]{1,0:T(8,128)(2,1)S(1)}, u32[]{:S(2)}, u32[]{:S(2)}) collective-permute-start(bf16[224,512]{1,0:T(8,128)(2,1)S(1)} %bitcast.16), channel_id=1, source_target_pairs={{0,31},{1,0},{2,1},{3,2},{4,3},{5,4},{6,5},{7,6},{8,7},{9,8},{10,9... | collective-permute-start | bytes 688136 | tf_op jit(solution)/shard_map/ppermute | solution.py:557
  158.7 0.7 copy-start.6
  158.7 0.8 copy-start.8
  181.4 10.3 %collective-permute-start.7 = (bf16[2,112,512]{2,1,0:T(8,128)(2,1)S(1)}, bf16[2,112,512]{2,1,0:T(8,128)(2,1)S(1)}, u32[]{:S(2)}, u32[]{:S(2)}) collective-permute-start(bf16[2,112,512]{2,1,0:T(8,128)(2,1)S(1)} %get-tuple-element.12), channel_id=1, source_target_pairs={{0,1},{1,2},{2,3},{3,4},{4,5},{5,6},{6,7},{7,8},{8,9},{9,10},{10,1... | collective-permute-start | bytes 688136 | tf_op jit(solution)/shard_map/ppermute | solution.py:557
  181.5 10.2 %collective-permute-start.8 = (bf16[2,112,512]{2,1,0:T(8,128)(2,1)S(1)}, bf16[2,112,512]{2,1,0:T(8,128)(2,1)S(1)}, u32[]{:S(2)}, u32[]{:S(2)}) collective-permute-start(bf16[2,112,512]{2,1,0:T(8,128)(2,1)S(1)} %get-tuple-element.11), channel_id=1, source_target_pairs={{0,31},{1,0},{2,1},{3,2},{4,3},{5,4},{6,5},{7,6},{8,7},{9,8},{10,9... | collective-permute-start | bytes 688136 | tf_op jit(solution)/shard_map/ppermute | solution.py:557
  191.7 0.7 copy-start.3
  192.4 0.7 copy-start.4
where the time goes:
time: 198 us
  Pallas kernels  141 us (71%)
  starting transfers between devices  25.5 us (13%)
  waiting for transfers between devices  19.8 us (10%)
  local copies, waits for them, and re-layouts  11.8 us (6%)
    pallas_call x1, Pallas kernels, swap(): pl.pallas_call(swap_kernel, out_shape=jax.ShapeDtypeStruct((64, MSG, D),...  43.7 us
    pallas_call x2, Pallas kernels, window_block(): pl.pallas_call(window_kernel, in_specs=[SMEM] + [VMEM] * 7, out_specs=VME...  41.7 us
    ppermute x8, starting transfers between devices, passed_along(): return lax.ppermute(value, axis, pairs)  25.5 us
    pallas_call x1, Pallas kernels, coarse_block(): pl.pallas_call(coarse_kernel, in_specs=[SMEM] + [VMEM] * 9, out_specs=VME...  21.5 us
    ppermute x8, waiting for transfers between devices, passed_along(): return lax.ppermute(value, axis, pairs)  15.9 us
    pallas_call x1, Pallas kernels, encode(): pl.pallas_call(encode_kernel, grid=(576 // CHUNK,), in_specs=[pl.BlockSpe...  12.5 us
    pallas_call x1, Pallas kernels, sort_fields(): pl.pallas_call(sort_kernel, grid=(levels,), in_specs=[SMEM, pl.BlockSpec(...  8.75 us
    pallas_call x1, Pallas kernels, settle(): pl.pallas_call(settle_kernel, in_specs=[VMEM] * 3, out_specs=VMEM, out_sh...  7.7 us
  transfers between devices with their start and end apart: 9, of which 5 were waited for; matrix products, arithmetic and copies ran while one was open for 0% of the time, Pallas kernels for 0%

commit v1 on v0

--- a/solution.py
+++ b/solution.py
@@ -54,32 +54,39 @@
     return jnp.where(condition, 1.0, 0.0).astype(BF)
 
 
-def group_ids(first_column):
-    ids = np.full((4, 56), FAR, np.float32)
+def group_ids(first_column, spare=None):
+    ids = np.zeros((4, 56), np.float32)
     for sub in range(4):
-        for q in range(54):
-            column = first_column + 2 * (q // 18) + (sub & 1)
-            ids[sub, q] = column * 36 + (2 * (q % 6) + (sub >> 1)) * 3 + q % 18 // 6
+        for q in range(56):
+            p = min(q, 53)
+            column = first_column + 2 * (p // 18) + (sub & 1)
+            ids[sub, q] = column * 36 + (2 * (p % 6) + (sub >> 1)) * 3 + p % 18 // 6
+    if spare is not None:
+        ids[:, 54:] = spare
     return ids
 
 
-def half_ids(band, first_column):
-    ids = np.full((112,), 2 * FAR, np.float32)
-    for q in range(108):
-        ids[q] = (first_column + q // 18) * 36 + (band * 6 + q % 6) * 3 + q % 18 // 6
+def half_ids(band, first_column, spare=None):
+    ids = np.zeros((112,), np.float32)
+    for q in range(112):
+        p = min(q, 107)
+        ids[q] = (first_column + p // 18) * 36 + (band * 6 + p % 6) * 3 + p % 18 // 6
+    if spare is not None:
+        ids[108:] = spare
     return ids
 
 
 def tables():
-    spread = np.concatenate([group_ids(6 * g).reshape(-1) for g in range(-1, 5)])
+    groups = [group_ids(6 * g, FAR).reshape(-1) for g in range(-1, 5)]
+    spread = np.concatenate(groups[1:5] + [groups[0], groups[5]])
     windows = np.concatenate(
         [np.concatenate([half_ids(b, 0), half_ids(b, 6)]) for _ in range(2) for b in range(2)]
     )
     held = np.zeros((8, 1344), np.float32)
     held[0] = np.concatenate(
-        [windows]
-        + [half_ids(b, 6 - PLON) for b in range(2)]
-        + [half_ids(b, PLON) for b in range(2)]
+        [np.concatenate([half_ids(b, 0, FAR), half_ids(b, 6, FAR)]) for _ in range(2) for b in range(2)]
+        + [half_ids(b, 6 - PLON, FAR) for b in range(2)]
+        + [half_ids(b, PLON, FAR) for b in range(2)]
     )
     held[1, :448] = 1.0
     by_sub = np.stack([group_ids(6 * g) for g in range(4)], axis=1).reshape(-1)
@@ -371,120 +378,205 @@
     return offsets * lax.rsqrt(spread + epsilon)
 
 
-def heads_of_group(qkv, out, rows, g, width, bias):
-    column = pl.multiple_of(g * 128, 128)
-    q = qkv[rows, pl.ds(column, 128)]
-    k = qkv[rows, pl.ds(width + column, 128)]
-    v = qkv[rows, pl.ds(2 * width + column, 128)]
-    v = jnp.concatenate([v, jnp.ones_like(v)], axis=1)
+def heads_of_group(qkv, out, g, width, valid):
+    column = g * 128
+    if not isinstance(g, int):
+        column = pl.multiple_of(column, 128)
+    q = qkv[:, pl.ds(column, 128)]
+    k = qkv[:, pl.ds(width + column, 128)]
+    v = qkv[:, pl.ds(2 * width + column, 128)]
+    v = jnp.concatenate([v * valid, valid], axis=1)
     head = div(iota((1, 128), 1), 32.0)
-    scale = math.log2(math.e) / math.sqrt(32.0)
-    total = jnp.zeros((224, 128), F32)
-    for h in range(4):
-        only = head == float(h)
-        scores = dot_nt(q * hot(only), k) + bias
-        peak = jnp.max(scores, axis=1, keepdims=True)
-        weights = jnp.exp2((scores - peak) * scale).astype(BF)
-        mixed = dot(weights, v)
-        total = total + jnp.where(only, mixed[:, :128] / mixed[:, 128:], 0.0)
-    out[rows, pl.ds(column, 128)] = total.astype(BF)
-
-
-def key_bias(slots, valid):
-    lane = iota((1, 224), 1)
-    lane = lane - slots * div(lane, float(slots))
-    return jnp.where(lane < valid, 0.0, -1.0e30)
-
-
-def shift_starts(shift_ref):
-    s = shift_ref[0]
+    queries = jnp.concatenate([q * hot(head == float(h)) for h in range(4)], axis=0)
+    scores = dot_nt(queries, k)
+    scores = (scores - jnp.max(scores, axis=1, keepdims=True)) * (math.log2(math.e) / math.sqrt(32.0))
+    mixed = dot(jnp.exp2(scores).astype(BF), v)
+    head = jnp.concatenate([head, head], axis=1)
+    total = mixed[0:224]
+    for h in range(1, 4):
+        total = jnp.where(head == float(h), mixed[h * 224 : (h + 1) * 224], total)
+    out[:, pl.ds(column, 128)] = (total[:, :128] / total[:, 128:]).astype(BF)
+
+
+def valid_keys(slots, valid):
+    row = iota((224, 128), 0)
+    return hot(row - slots * div(row, float(slots)) < valid)
+
+
+def shift_starts(s):
     near = s.astype(F32)
     far = jnp.where(s <= 6, s + 12, s - 12).astype(F32)
     return near, far
 
 
-def window_kernel(
-    shift_ref, before_ref, own_ref, after_ref, spread_ref, windows_ref, w_ref, proj_ref, out_ref, cells, x, qkv, mixed
-):
-    near, far = shift_starts(shift_ref)
-    cells[0:224, :] = before_ref[...]
-    for g in range(4):
-        cells[(g + 1) * 224 : (g + 2) * 224, :] = own_ref[g]
-    cells[1120:1344, :] = after_ref[...]
-    for n in range(4):
-        rows = slice(n * 224, (n + 1) * 224)
-        target = windows_ref[rows, :] + 36.0 * (near if n < 2 else far)
-        x[rows, :] = dot(hot(target == spread_ref[...]), cells[...]).astype(BF)
-    for n in range(4):
-        rows = slice(n * 224, (n + 1) * 224)
-        normed = normalize(x[rows, :].astype(F32)).astype(BF)
-        qkv[rows, :] = dot(normed, w_ref[...]).astype(BF)
-    bias = key_bias(112, 108)
-
-    @pl.loop(0, 16)
+class Links:
+    def __init__(self, send, recv):
+        lev = lax.axis_index("lev")
+        win = lax.axis_index("win")
+        self.send, self.recv = send, recv
+        self.sides = (
+            (lev, lax.rem(win + N_WIN - 1, N_WIN)),
+            (lev, lax.rem(win + 1, N_WIN)),
+        )
+
+    def greet(self):
+        barrier = pltpu.get_barrier_semaphore()
+        for side in self.sides:
+            pl.semaphore_signal(barrier, inc=1, device_id=side, device_id_type=MESH)
+        pl.semaphore_wait(barrier, 2)
+
+    def copy(self, side, sem, source, target):
+        return pltpu.make_async_remote_copy(
+            src_ref=source,
+            dst_ref=target,
+            send_sem=self.send.at[sem],
+            recv_sem=self.recv.at[sem],
+            device_id=self.sides[side],
+            device_id_type=MESH,
+        )
+
+    def cells(self, base, own, halo):
+        return (
+            self.copy(0, base, own.at[pl.ds(0, 224)], halo.at[pl.ds(224, 224)]),
+            self.copy(1, base + 1, own.at[pl.ds(672, 224)], halo.at[pl.ds(0, 224)]),
+        )
+
+    def results(self, base, band, results, land):
+        first = pl.multiple_of(448 + band * 224, 16)
+        return (
+            self.copy(
+                0,
+                base + 2 * band,
+                results.at[pl.ds(first, 112)],
+                land.at[pl.ds(pl.multiple_of(224 + band * 112, 16), 112)],
+            ),
+            self.copy(
+                1,
+                base + 2 * band + 1,
+                results.at[pl.ds(pl.multiple_of(first + 112, 16), 112)],
+                land.at[pl.ds(pl.multiple_of(band * 112, 16), 112)],
+            ),
+        )
+
+
+def shifted_windows(links, base, shift, own, halo, results, land, spread_ref, windows_ref, w_ref, proj_ref, x, qkv, mixed):
+    near, far = shift_starts(shift)
+    valid = valid_keys(112, 108)
+
+    @pl.loop(0, 4)
     def _(step):
-        rows = pl.ds(pl.multiple_of((step // 4) * 224, 224), 224)
-        heads_of_group(qkv, mixed, rows, lax.rem(step, 4), D, bias)
-
-    for n in range(4):
-        rows = slice(n * 224, (n + 1) * 224)
-        out_ref[n] = (x[rows, :].astype(F32) + dot(mixed[rows, :], proj_ref[...])).astype(BF)
-
-
-def window_block(shift, before, own, after, spread, windows, w_qkv, w_proj):
-    return pl.pallas_call(
-        window_kernel,
-        in_specs=[SMEM] + [VMEM] * 7,
-        out_specs=VMEM,
-        out_shape=jax.ShapeDtypeStruct((4, 224, D), BF),
-        scratch_shapes=[
-            pltpu.VMEM((1344, D), BF),
-            pltpu.VMEM((896, D), BF),
-            pltpu.VMEM((896, 3 * D), BF),
-            pltpu.VMEM((896, D), BF),
-        ],
-        compiler_params=params(),
-        name="window_block",
-    )(shift, before, own, after, spread, windows, w_qkv, w_proj)
-
-
-def held_ids(shift_ref, held_ref):
-    near, far = shift_starts(shift_ref)
-    local = held_ref[1:2, :]
-    return held_ref[0:1, :] + 36.0 * jnp.where(local > 0.5, near, far)
-
-
-def gather_cells(cells, own_ref, before_ref, after_ref):
-    for n in range(4):
-        cells[n * 224 : (n + 1) * 224, :] = own_ref[n]
-    for b in range(2):
-        cells[896 + b * 112 : 1008 + b * 112, :] = before_ref[b]
-        cells[1120 + b * 112 : 1232 + b * 112, :] = after_ref[b]
-
-
-def coarse_kernel(
+        band = step // 2
+        outer = lax.rem((step + 1) // 2, 2)
+        rows = pl.ds(pl.multiple_of((outer * 2 + band) * 224, 224), 224)
+        target = windows_ref[rows, :] + 36.0 * jnp.where(outer == 0, near, far)
+        x[...] = dot(hot(target == spread_ref[:, 0:896]), own[...])
+
+        @pl.when(step == 1)
+        def _():
+            for copy in links.cells(base, own, halo):
+                copy.wait()
+
+        @pl.when(outer == 1)
+        def _():
+            x[...] += dot(hot(target == spread_ref[:, 896:1344]), halo[...])
+
+        qkv[...] = dot(normalize(x[...]).astype(BF), w_ref[...]).astype(BF)
+        for g in range(4):
+            heads_of_group(qkv, mixed, g, D, valid)
+        results[rows, :] = (x[...] + dot(mixed[...], proj_ref[...])).astype(BF)
+
+        @pl.when(outer == 1)
+        def _():
+            for copy in links.results(base + 2, band, results, land):
+                copy.start()
+
+
+def held_ids(shift, held_ref):
+    near, far = shift_starts(shift)
+    return held_ref[0:1, :] + 36.0 * jnp.where(held_ref[1:2, :] > 0.5, near, far)
+
+
+def gathered(target, ids, results, land):
+    return dot(hot(target == ids[:, 0:896]), results[...]) + dot(
+        hot(target == ids[:, 896:1344]), land[...]
+    )
+
+
+def unet_kernel(
     shift_ref,
     own_ref,
-    before_ref,
-    after_ref,
+    spread_ref,
+    windows_ref,
     held_ref,
     sub_ref,
-    merge_ref,
-    w_ref,
-    proj_ref,
-    expand_ref,
+    final_ref,
+    qkv_a,
+    proj_a,
+    merge_w,
+    qkv_b,
+    proj_b,
+    expand_w,
+    qkv_c,
+    proj_c,
     out_ref,
-    cells,
+    qkv_a_v,
+    proj_a_v,
+    merge_v,
+    qkv_b_v,
+    proj_b_v,
+    expand_v,
+    qkv_c_v,
+    proj_c_v,
+    halo_a,
+    halo_c,
+    land_a,
+    land_c,
+    results,
+    joined,
     first,
+    x,
     qkv,
     mixed,
+    qkv_wide,
+    mixed_wide,
+    send,
+    recv,
+    weight_sem,
 ):
-    gather_cells(cells, own_ref, before_ref, after_ref)
-    ids = held_ids(shift_ref, held_ref)
+    links = Links(send, recv)
+    links.greet()
+    for copy in links.cells(0, own_ref, halo_a):
+        copy.start()
+    pairs = [
+        (qkv_a, qkv_a_v),
+        (proj_a, proj_a_v),
+        (merge_w, merge_v),
+        (qkv_b, qkv_b_v),
+        (proj_b, proj_b_v),
+        (expand_w, expand_v),
+        (qkv_c, qkv_c_v),
+        (proj_c, proj_c_v),
+    ]
+    loads = [pltpu.make_async_copy(a, b, weight_sem.at[n]) for n, (a, b) in enumerate(pairs)]
+    for load in loads:
+        load.start()
+    loads[0].wait()
+    loads[1].wait()
+    shift = shift_ref[0]
+    shifted_windows(
+        links, 0, shift, own_ref, halo_a, results, land_a, spread_ref, windows_ref, qkv_a_v, proj_a_v, x, qkv, mixed
+    )
+    for load in loads[2:]:
+        load.wait()
+    for band in range(2):
+        for copy in links.results(2, band, results, land_a):
+            copy.wait()
+
+    ids = held_ids(shift, held_ref)
     total = jnp.zeros((224, 1), F32)
     for sub in range(4):
         rows = slice(sub * 224, (sub + 1) * 224)
-        piece = dot(hot(sub_ref[rows, :] == ids), cells[...])
+        piece = gathered(sub_ref[rows, :], ids, results, land_a)
         first[rows, :] = piece.astype(BF)
         total = total + jnp.sum(piece, axis=1, keepdims=True)
     centre = total * (1.0 / (4 * D))
@@ -496,69 +588,54 @@
     down = jnp.zeros((224, 2 * D), F32)
     for sub in range(4):
         offsets = first[sub * 224 : (sub + 1) * 224, :].astype(F32) - centre
-        down = down + dot((offsets * scale).astype(BF), merge_ref[sub * D : (sub + 1) * D, :])
+        down = down + dot((offsets * scale).astype(BF), merge_v[sub * D : (sub + 1) * D, :])
     down = down.astype(BF).astype(F32)
-    qkv[...] = dot(normalize(down).astype(BF), w_ref[...]).astype(BF)
-    bias = key_bias(56, 54)
-
-    @pl.loop(0, 8)
-    def _(g):
-        heads_of_group(qkv, mixed, pl.ds(0, 224), g, 2 * D, bias)
-
-    coarse = (down + dot(mixed[...], proj_ref[...])).astype(BF).astype(F32)
+    qkv_wide[...] = dot(normalize(down).astype(BF), qkv_b_v[...]).astype(BF)
+    valid = valid_keys(56, 54)
+
+    @pl.loop(0, 2)
+    def _(step):
+        for g in range(4):
+            heads_of_group(qkv_wide, mixed_wide, step * 4 + g, 2 * D, valid)
+
+    coarse = (down + dot(mixed_wide[...], proj_b_v[...])).astype(BF).astype(F32)
     normed = normalize(coarse).astype(BF)
     for sub in range(4):
-        grown = dot(normed, expand_ref[:, sub * D : (sub + 1) * D])
-        joined = grown + first[sub * 224 : (sub + 1) * 224, :].astype(F32)
+        grown = dot(normed, expand_v[:, sub * D : (sub + 1) * D])
+        grown = grown + first[sub * 224 : (sub + 1) * 224, :].astype(F32)
         for g in range(4):
-            out_ref[g, sub] = joined[g * 56 : (g + 1) * 56, :].astype(BF)
-
-
-def coarse_block(shift, own, before, after, held, by_sub, merge_w, w_qkv, w_proj, expand_w):
-    return pl.pallas_call(
-        coarse_kernel,
-        in_specs=[SMEM] + [VMEM] * 9,
-        out_specs=VMEM,
-        out_shape=jax.ShapeDtypeStruct((4, 4, 56, D), BF),
-        scratch_shapes=[
-            pltpu.VMEM((1344, D), BF),
-            pltpu.VMEM((896, D), BF),
-            pltpu.VMEM((224, 6 * D), BF),
-            pltpu.VMEM((224, 2 * D), BF),
-        ],
-        compiler_params=params(),
-        name="coarse_block",
-    )(shift, own, before, after, held, by_sub, merge_w, w_qkv, w_proj, expand_w)
-
-
-def final_kernel(shift_ref, own_ref, before_ref, after_ref, held_ref, final_ref, out_ref, cells):
-    gather_cells(cells, own_ref, before_ref, after_ref)
-    ids = held_ids(shift_ref, held_ref)
+            joined[g * 224 + sub * 56 : g * 224 + (sub + 1) * 56, :] = grown[g * 56 : (g + 1) * 56, :].astype(BF)
+
+    for copy in links.cells(6, joined, halo_c):
+        copy.start()
+    shift = shift_ref[1]
+    shifted_windows(
+        links, 6, shift, joined, halo_c, results, land_c, spread_ref, windows_ref, qkv_c_v, proj_c_v, x, qkv, mixed
+    )
+    for band in range(2):
+        for copy in links.results(8, band, results, land_c):
+            copy.wait()
+    ids = held_ids(shift, held_ref)
     for b in range(4):
         rows = slice(b * 216, (b + 1) * 216)
-        out_ref[rows, :] = dot(hot(final_ref[rows, :] == ids), cells[...]).astype(BF)
-
-
-def final_order(shift, own, before, after, held, final):
+        out_ref[rows, :] = gathered(final_ref[rows, :], ids, results, land_c).astype(BF)
+
+
+def unet(shifts, grid, weights):
+    rows = lambda count, width=D: pltpu.VMEM((count, width), BF)
     return pl.pallas_call(
-        final_kernel,
-        in_specs=[SMEM] + [VMEM] * 5,
+        unet_kernel,
+        in_specs=[SMEM] + [VMEM] * 6 + [ANY] * 8,
         out_specs=VMEM,
         out_shape=jax.ShapeDtypeStruct((PLAT * LATENT * PLON, D), BF),
-        scratch_shapes=[pltpu.VMEM((1344, D), BF)],
-        compiler_params=params(),
-        name="final_order",
-    )(shift, own, before, after, held, final)
-
-
-def passed_along(value, axis, steps):
-    count = lax.axis_size(axis)
-    pairs = [(source, (source + steps) % count) for source in range(count)]
-    return lax.ppermute(value, axis, pairs)
-
-
-def from_sides(to_previous, to_next):
-    return passed_along(to_next, "win", 1), passed_along(to_previous, "win", -1)
+        scratch_shapes=[pltpu.VMEM(w.shape, BF) for w in weights]
+        + [rows(448)] * 4
+        + [rows(896)] * 3
+        + [pltpu.VMEM((224, D), F32), rows(224, 3 * D), rows(224), rows(224, 6 * D), rows(224, 2 * D)]
+        + [pltpu.SemaphoreType.DMA((12,)), pltpu.SemaphoreType.DMA((12,)), pltpu.SemaphoreType.DMA((8,))],
+        compiler_params=params(collective_id=1, has_side_effects=True),
+        name="unet",
+    )(shifts, grid, *tables(), *weights)
 
 
 def local(
@@ -579,7 +656,6 @@
 ):
     lev_at = lax.axis_index("lev")
     win_at = lax.axis_index("win")
-    spread, windows, held, by_sub, final = tables()
     slots = lax.dynamic_slice_in_dim(patch_order, win_at * PSH, PSH, 0).reshape(1, PSH)
     core = lax.rem(lev_at, 2).astype(jnp.int32).reshape(1)
     keep, send, meta = sort_fields(core, slots, fields)
@@ -588,19 +664,8 @@
     arrived = swap(messages.reshape(64, MSG, D)).reshape(2, 32 * MSG, D)
     grid = settle(arrived, latent_query, enc_out)
 
-    def shifted(grid, shift, w_qkv, w_proj):
-        before, after = from_sides(grid[0], grid[3])
-        done = window_block(shift, before, grid, after, spread, windows, w_qkv, w_proj)
-        return (done,) + from_sides(done[2:, :112], done[2:, 112:])
-
-    shift = shift_offsets[0:1]
-    done, before, after = shifted(grid, shift, qkv_a, proj_a)
-    joined = coarse_block(
-        shift, done, before, after, held, by_sub, merge_w, qkv_b, proj_b, expand_w
-    ).reshape(4, 224, D)
-    shift = shift_offsets[1:2]
-    done, before, after = shifted(joined, shift, qkv_c, proj_c)
-    result = final_order(shift, done, before, after, held, final)
+    weights = (qkv_a, proj_a, merge_w, qkv_b, proj_b, expand_w, qkv_c, proj_c)
+    result = unet(shift_offsets, grid.reshape(896, D), weights)
     return result.reshape(PLAT, LATENT, PLON, D).transpose(0, 2, 1, 3)
 
 

time: 198 us -> 140 us (0.71)
  starting transfers between devices: 25.5 us -> 0.01 us
  waiting for transfers between devices: 19.8 us -> 3.9 us
  Pallas kernels: 141 us -> 131 us
  local copies, waits for them, and re-layouts: 11.8 us -> 4.77 us
    ppermute x8 -> x0, starting transfers between devices: 25.5 us -> none  [passed_along(): return lax.ppermute(value, axis, pairs)]
    ppermute x8 -> x0, waiting for transfers between devices: 15.9 us -> none  [passed_along(): return lax.ppermute(value, axis, pairs)]
    pallas_call x4 -> x1, Pallas kernels: 67.9 us -> 58 us  [unet(): pl.pallas_call(unet_kernel, in_specs=[SMEM] + [VMEM] * 6 + [ANY] * 8, out...]
    slice x4 -> x0, local copies, waits for them, and re-layouts: 3.83 us -> none  [the longest x2 2.16 us: shifted(): return (done,) + from_sides(done[2:, :112], done[2:, 112:])]
    unnamed x20 -> x3, local copies, waits for them, and re-layouts: 5.51 us -> 3.39 us
  transfers between devices with their start and end apart: 9 -> 1, of which waited for: 5 -> 1; matrix products, arithmetic and copies ran while one was open for 0% -> 0% of each run, Pallas kernels for 0% -> 0%
where the time goes in v1:
time: 140 us; the launch traced here: 139 us
  Pallas kernels  131 us (94%)
  local copies, waits for them, and re-layouts  4.77 us (3%)
  waiting for transfers between devices  3.9 us (3%)
    pallas_call x1, Pallas kernels, unet(): pl.pallas_call(unet_kernel, in_specs=[SMEM] + [VMEM] * 6 + [ANY] * 8, out...  58 us
    pallas_call x1, Pallas kernels, swap(): pl.pallas_call(swap_kernel, out_shape=jax.ShapeDtypeStruct((64, MSG, D),...  43.6 us
    pallas_call x1, Pallas kernels, encode(): pl.pallas_call(encode_kernel, grid=(576 // CHUNK,), in_specs=[pl.BlockSpe...  12.5 us
    pallas_call x1, Pallas kernels, sort_fields(): pl.pallas_call(sort_kernel, grid=(levels,), in_specs=[SMEM, pl.BlockSpec(...  8.82 us
    pallas_call x1, Pallas kernels, settle(): pl.pallas_call(settle_kernel, in_specs=[VMEM] * 3, out_specs=VMEM, out_sh...  7.67 us
    ppermute x1, waiting for transfers between devices, local(): got = lax.ppermute(send, 'lev', [(0, 1), (1, 0), (2, 3), (3, 2)])  3.9 us
    unnamed x3, local copies, waits for them, and re-layouts  3.39 us
  transfers between devices with their start and end apart: 1, of which 1 were waited for; matrix products, arithmetic and copies ran while one was open for 0% of the time, Pallas kernels for 0%

profile of v1, /device:TPU:0, one launch (start us, length us, event | category | flops | bytes accessed | tf_op | source)
XLA Modules:
  0.0 139.3 jit_solution(16669402520677602285)
XLA Ops:
  0.0 0.8 dynamic_slice.3
  0.8 0.6 reshape.19.slots_ref
  1.4 8.8 %sort_fields.1 = (bf16[3,576,512]{2,1,0:T(8,128)(2,1)}, bf16[3,576,512]{2,1,0:T(8,128)(2,1)}, bf16[576,128]{1,0:T(8,128)(2,1)}) custom-call(s32[1]{0:T(128)} %bitcast.core_ref, s32[1,1152]{1,0:T(1,128)} %reshape.19.slots_ref, bf16[3,1152,512]{2,1,0:T(8,128)(2,1)} %x_ref.1), custom_call_target="tpu_custom_call" | custom-call | tf_op jit(solution)/shard_map/sort_fields/pallas_call | solution.py:151
  10.2 0.0 collective-permute-start
  10.2 3.9 %collective-permute-done.got_ref = bf16[3,576,512]{2,1,0:T(8,128)(2,1)S(1)} collective-permute-done((bf16[3,576,512]{2,1,0:T(8,128)(2,1)}, bf16[3,576,512]{2,1,0:T(8,128)(2,1)S(1)}, u32[]{:S(2)}, u32[]{:S(2)}) %collective-permute-start) | collective-permute-done | bytes 1769504 | tf_op jit(solution)/shard_map/ppermute | solution.py:662
  14.1 0.0 copy-start
  14.1 1.3 copy-done
  15.4 12.5 %encode.1 = bf16[2048,512]{1,0:T(8,128)(2,1)} custom-call(bf16[3,576,512]{2,1,0:T(8,128)(2,1)} %get-tuple-element.8.own_ref, bf16[3,576,512]{2,1,0:T(8,128)(2,1)} %copy-done, bf16[576,128]{1,0:T(8,128)(2,1)} %get-tuple-element.10.meta_ref, bf16[512,1024]{1,0:T(8,128)(2,1)} %kv_ref.1, bf16[3,512]{1,0:T(4,128)(2,1)} %query_ref.3), custom_call_target="tpu_custom_call" | custom-call | tf_op jit(solution)/shard_map/encode/pallas_call | solution.py:244
  27.9 43.6 %swap.1 = bf16[64,32,512]{2,1,0:T(8,128)(2,1)} custom-call(bf16[64,32,512]{2,1,0:T(8,128)(2,1)} %bitcast.7), custom_call_target="tpu_custom_call" | custom-call | tf_op jit(solution)/shard_map/swap/pallas_call | solution.py:313
  71.4 7.7 %settle.1 = bf16[4,224,512]{2,1,0:T(8,128)(2,1)} custom-call(bf16[2,1024,512]{2,1,0:T(8,128)(2,1)} %bitcast.8, bf16[3,512]{1,0:T(4,128)(2,1)} %query_ref.3, bf16[512,512]{1,0:T(8,128)(2,1)} %out_w_ref.1), custom_call_target="tpu_custom_call" | custom-call | tf_op jit(solution)/shard_map/settle/pallas_call | solution.py:364
  79.1 58.0 %unet.1 = bf16[864,512]{1,0:T(8,128)(2,1)} custom-call(s32[2]{0:T(128)} %shift_ref.1, bf16[896,512]{1,0:T(8,128)(2,1)} %bitcast.9, f32[1,1344]{1,0:T(1,128)} %constant.29.clone.spread_ref, f32[896,1]{1,0:T(8,128)} %constant.30.clone.windows_ref, f32[8,1344]{1,0:T(8,128)} %constant.31.clone.held_ref, f32[896,1]{1,0:T(8,128)} %constant.32.clone.sub_ref, ...), custom_call_target="tpu_custom_call" | custom-call | tf_op jit(solution)/shard_map/unet/pallas_call | solution.py:626
  137.1 2.1 %copy.21 = bf16[12,24,3,512]{3,1,2,0:T(8,128)(2,1)} copy(bf16[12,24,3,512]{3,1,2,0:T(8,128)(2,1)} %bitcast.10) | data formatting | bytes 1769472
Async XLA Ops:
  10.2 3.9 %collective-permute-start = (bf16[3,576,512]{2,1,0:T(8,128)(2,1)}, bf16[3,576,512]{2,1,0:T(8,128)(2,1)S(1)}, u32[]{:S(2)}, u32[]{:S(2)}) collective-permute-start(bf16[3,576,512]{2,1,0:T(8,128)(2,1)} %get-tuple-element.9), channel_id=1, source_target_pairs={{0,32},{32,0},{64,96},{96,64},{1,33},{33,1},{65,97},{97,65},{2,34}... | collective-permute-start | bytes 5308424 | tf_op jit(solution)/shard_map/ppermute | solution.py:662
  14.1 1.3 copy-start

commit v2 on v1

--- a/solution.py
+++ b/solution.py
@@ -28,6 +28,7 @@
 VMEM = pl.BlockSpec(memory_space=pltpu.VMEM)
 SMEM = pl.BlockSpec(memory_space=pltpu.SMEM)
 ANY = pl.BlockSpec(memory_space=pl.ANY)
+HBM = pl.BlockSpec(memory_space=pltpu.HBM)
 
 
 def params(mib=60, **more):
@@ -104,111 +105,166 @@
     )
 
 
-def sort_kernel(core_ref, slots_ref, x_ref, keep_ref, send_ref, meta_ref, perm):
-    @pl.when(pl.program_id(0) == 0)
-    def _():
-        core = core_ref[0].astype(F32)
-        p = slots_ref[...].astype(F32)
-        row = div(p, 768.0)
-        column = p - row * 768.0
-        band = div(row, 12.0)
-        shard = div(column, 24.0)
-        row = row - band * 12.0
-        column = column - shard * 24.0
-        half = div(band, 2.0)
-        other = jnp.abs(band - 2.0 * half - core)
-        key = other * 64.0 + half * 32.0 + shard
-        member = hot(iota((128, PSH), 0) == key)
-        upper = hot(iota((128, 128), 0) < iota((128, 128), 1))
-        seen = jnp.zeros((128, 1), F32)
-        ranks = []
-        for b in range(PSH // 128):
-            piece = member[:, b * 128 : (b + 1) * 128]
-            wide = piece.astype(F32)
-            ranks.append(jnp.sum(wide * (dot(piece, upper) + seen), axis=0, keepdims=True))
-            seen = seen + jnp.sum(wide, axis=1, keepdims=True)
-        target = key * PER + jnp.concatenate(ranks, axis=1)
-        for b in range(PSH // 128):
-            perm[b * 128 : (b + 1) * 128, :] = hot(iota((128, PSH), 0) + b * 128.0 == target)
-        j = div(column, 2.0)
-        group = div(j, 3.0)
-        i = div(row, 2.0)
-        sub = 2.0 * (row - 2.0 * i) + column - 2.0 * j
-        base = group * 224.0 + sub * 56.0 + (j - 3.0 * group) * 18.0 + i
-        high = div(base, 16.0)
-        low = base - 16.0 * high
-        at = iota((128, PSH), 0)
-        meta = jnp.where(at == 48.0, high, jnp.where(at == 49.0, low, 0.0)).astype(BF)
-        meta_ref[...] = dot_nt(perm[0:576, :], meta).astype(BF)
-
-    done = dot(perm[...], x_ref[0])
-    keep_ref[0] = done[:576].astype(BF)
-    send_ref[0] = done[576:].astype(BF)
-
-
-def sort_fields(core, slots, fields):
-    levels = fields.shape[0]
+def place_of_me():
+    lev = lax.axis_index("lev")
+    win = lax.axis_index("win")
+    return lev // 2, win // 8, lax.rem(win // 4, 2), lax.rem(win, 4), lax.rem(lev, 2)
+
+
+def receiver(j):
+    half, x, low, y, core = place_of_me()
+    k = lax.rem(((j // 16) * 8 + lax.rem(j, 8)) * 11, 32)
+    half = lax.rem(half + lax.rem(j // 8, 2), 2)
+    x = lax.rem(x + k // 8, 4)
+    low = lax.rem(low + lax.rem(k // 4, 2), 2)
+    y = lax.rem(y + lax.rem(k, 4), 4)
+    return (half * 2 + core, x * 8 + low * 4 + y)
+
+
+def message_of(half, shard):
+    my_half, my_x, my_low, my_y, _ = (value.astype(F32) for value in place_of_me())
+    x = div(shard, 8.0)
+    y = shard - 8.0 * x
+    low = div(y, 4.0)
+    y = y - 4.0 * low
+    x = x - my_x + 4.0
+    x = x - 4.0 * div(x, 4.0)
+    y = y - my_y + 4.0
+    y = y - 4.0 * div(y, 4.0)
+    pair = 3.0 * (8.0 * x + 4.0 * jnp.abs(low - my_low) + y)
+    pair = pair - 32.0 * div(pair, 32.0)
+    block = div(pair, 8.0)
+    return block * 16.0 + 8.0 * jnp.abs(half - my_half) + pair - 8.0 * block
+
+
+def sort_kernel(
+    order_ref, fields_ref, keep_ref, got_ref, meta_ref, perm, fields, outgoing, load_sem, send_sem, recv_sem
+):
+    lev = lax.axis_index("lev")
+    win = lax.axis_index("win")
+    mate = (lev + 1 - 2 * lax.rem(lev, 2), win)
+    loads = [
+        pltpu.make_async_copy(fields_ref.at[l], fields.at[l], load_sem.at[l]) for l in range(3)
+    ]
+    for load in loads:
+        load.start()
+    barrier = pltpu.get_barrier_semaphore()
+    pl.semaphore_signal(barrier, inc=1, device_id=mate, device_id_type=MESH)
+
+    core = lax.rem(lev, 2).astype(F32)
+    p = jnp.concatenate([order_ref[pl.ds(9 * win + r, 1), :] for r in range(9)], axis=1).astype(F32)
+    row = div(p, 768.0)
+    column = p - row * 768.0
+    band = div(row, 12.0)
+    shard = div(column, 24.0)
+    row = row - band * 12.0
+    column = column - shard * 24.0
+    half = div(band, 2.0)
+    key = jnp.abs(band - 2.0 * half - core) * 64.0 + message_of(half, shard)
+    member = hot(iota((128, PSH), 0) == key)
+    upper = hot(iota((128, 128), 0) < iota((128, 128), 1))
+    seen = jnp.zeros((128, 1), F32)
+    ranks = []
+    for b in range(PSH // 128):
+        piece = member[:, b * 128 : (b + 1) * 128]
+        wide = piece.astype(F32)
+        ranks.append(jnp.sum(wide * (dot(piece, upper) + seen), axis=0, keepdims=True))
+        seen = seen + jnp.sum(wide, axis=1, keepdims=True)
+    target = key * PER + jnp.concatenate(ranks, axis=1)
+    for b in range(PSH // 128):
+        perm[b * 128 : (b + 1) * 128, :] = hot(iota((128, PSH), 0) + b * 128.0 == target)
+    pl.semaphore_wait(barrier, 1)
+    copies = []
+    for l in range(3):
+        loads[l].wait()
+        outgoing[l] = dot(perm[576:, :], fields[l]).astype(BF)
+        copies.append(
+            pltpu.make_async_remote_copy(
+                src_ref=outgoing.at[l],
+                dst_ref=got_ref.at[l],
+                send_sem=send_sem.at[l],
+                recv_sem=recv_sem.at[l],
+                device_id=mate,
+                device_id_type=MESH,
+            )
+        )
+        copies[l].start()
+    for l in range(3):
+        keep_ref[l] = dot(perm[:576, :], fields[l]).astype(BF)
+    j = div(column, 2.0)
+    group = div(j, 3.0)
+    i = div(row, 2.0)
+    sub = 2.0 * (row - 2.0 * i) + column - 2.0 * j
+    base = group * 224.0 + sub * 56.0 + (j - 3.0 * group) * 18.0 + i
+    high = div(base, 16.0)
+    low = base - 16.0 * high
+    at = iota((128, PSH), 0)
+    meta = jnp.where(at == 48.0, high, jnp.where(at == 49.0, low, 0.0)).astype(BF)
+    meta_ref[...] = dot_nt(perm[0:576, :], meta).astype(BF)
+    for copy in copies:
+        copy.wait()
+
+
+def sort_fields(order, fields):
+    levels = pltpu.VMEM((3, 576, D), BF)
     return pl.pallas_call(
         sort_kernel,
-        grid=(levels,),
-        in_specs=[
-            SMEM,
-            pl.BlockSpec((1, PSH), lambda l: (0, 0)),
-            pl.BlockSpec((1, PSH, D), lambda l: (l, 0, 0)),
-        ],
-        out_specs=[
-            pl.BlockSpec((1, 576, D), lambda l: (l, 0, 0)),
-            pl.BlockSpec((1, 576, D), lambda l: (l, 0, 0)),
-            pl.BlockSpec((576, 128), lambda l: (0, 0)),
-        ],
+        in_specs=[VMEM, ANY],
+        out_specs=[VMEM, ANY, VMEM],
         out_shape=[
-            jax.ShapeDtypeStruct((levels, 576, D), BF),
-            jax.ShapeDtypeStruct((levels, 576, D), BF),
+            jax.ShapeDtypeStruct((3, 576, D), BF),
+            jax.ShapeDtypeStruct((3, 576, D), BF),
             jax.ShapeDtypeStruct((576, 128), BF),
         ],
-        scratch_shapes=[pltpu.VMEM((PSH, PSH), BF)],
-        compiler_params=params(),
+        scratch_shapes=[
+            pltpu.VMEM((PSH, PSH), BF),
+            pltpu.VMEM((3, PSH, D), BF),
+            levels,
+            pltpu.SemaphoreType.DMA((3,)),
+            pltpu.SemaphoreType.DMA((3,)),
+            pltpu.SemaphoreType.DMA((3,)),
+        ],
+        compiler_params=params(60, collective_id=2, has_side_effects=True),
         name="sort_fields",
-    )(core, slots, fields)
-
-
-def encode_kernel(own_ref, got_ref, meta_ref, kv_ref, query_ref, out_ref, score_w, spread_w, stat_w, pick, stack):
-    @pl.when(pl.program_id(0) == 0)
-    def _():
-        c = iota((128, D), 0)
-        lane = iota((128, D), 1)
-        a = div(c, 16.0)
-        q = query_ref[...].astype(F32)
-        chosen = jnp.where(a == 0.0, q[0:1], jnp.where(a == 1.0, q[1:2], q[2:3]))
-        mine = (c - 16.0 * a == div(lane, 32.0)) & (c < 48.0)
-        heads = jnp.where(mine, chosen, 0.0).astype(BF)
-        folded = dot_nt(kv_ref[:, :D], heads) * (1.0 / math.sqrt(D // HEADS))
-        high = folded.astype(BF)
-        score_w[:, 0:128] = high
-        score_w[:, 128:256] = (folded - high.astype(F32)).astype(BF)
-        for a in range(LATENT):
-            spread_w[:, a * D : (a + 1) * D] = hot(c == 16.0 * a + div(lane, 32.0))
-            s = iota((128, 128), 0)
-            t = iota((128, 128), 1)
-            t = t - 64.0 * div(t, 64.0)
-            for piece in range(3):
-                here = (t >= 16.0 * piece) & (t < 16.0 * piece + 16.0)
-                stat_w[piece * 128 : (piece + 1) * 128, a * 128 : (a + 1) * 128] = hot(
-                    here & (s == 16.0 * a + t - 16.0 * piece)
-                )
-            stat_w[384:512, a * 128 : (a + 1) * 128] = hot((t >= 48.0) & (t < 50.0) & (s == t))
-        lane = iota((1, 6 * CHUNK), 1)
-        kind = div(lane, float(CHUNK))
-        slot = lane - kind * CHUNK
-        stats = kind >= 3.0
-        a = jnp.where(stats, kind - 3.0, kind)
-        dest = div(slot, float(PER))
-        k = a * PER + slot - dest * PER
-        row = dest * MSG + jnp.where(stats, 27.0 + div(k, 8.0), k)
-        for b in range(4):
-            pick[b * 128 : (b + 1) * 128, :] = hot(iota((128, 6 * CHUNK), 0) + b * 128.0 == row)
-
-    xs = [own_ref[l] for l in range(3)] + [got_ref[l] for l in range(3)]
+    )(order, fields)
+
+
+def encode_tables(kv_ref, query_ref, score_w, spread_w, stat_w, pick):
+    c = iota((128, D), 0)
+    lane = iota((128, D), 1)
+    a = div(c, 16.0)
+    q = query_ref[...].astype(F32)
+    chosen = jnp.where(a == 0.0, q[0:1], jnp.where(a == 1.0, q[1:2], q[2:3]))
+    mine = (c - 16.0 * a == div(lane, 32.0)) & (c < 48.0)
+    heads = jnp.where(mine, chosen, 0.0).astype(BF)
+    folded = dot_nt(kv_ref[:, :D], heads) * (1.0 / math.sqrt(D // HEADS))
+    high = folded.astype(BF)
+    score_w[:, 0:128] = high
+    score_w[:, 128:256] = (folded - high.astype(F32)).astype(BF)
+    s = iota((128, 128), 0)
+    t = iota((128, 128), 1)
+    t = t - 64.0 * div(t, 64.0)
+    for a in range(LATENT):
+        spread_w[:, a * D : (a + 1) * D] = hot(c == 16.0 * a + div(lane, 32.0))
+        for piece in range(3):
+            here = (t >= 16.0 * piece) & (t < 16.0 * piece + 16.0)
+            stat_w[piece * 128 : (piece + 1) * 128, a * 128 : (a + 1) * 128] = hot(
+                here & (s == 16.0 * a + t - 16.0 * piece)
+            )
+        stat_w[384:512, a * 128 : (a + 1) * 128] = hot((t >= 48.0) & (t < 50.0) & (s == t))
+    lane = iota((1, 6 * CHUNK), 1)
+    kind = div(lane, float(CHUNK))
+    slot = lane - kind * CHUNK
+    stats = kind >= 3.0
+    a = jnp.where(stats, kind - 3.0, kind)
+    dest = div(slot, float(PER))
+    k = a * PER + slot - dest * PER
+    row = dest * MSG + jnp.where(stats, 27.0 + div(k, 8.0), k)
+    for b in range(4):
+        pick[b * 128 : (b + 1) * 128, :] = hot(iota((128, 6 * CHUNK), 0) + b * 128.0 == row)
+
+
+def encode_chunk(xs, meta, kv_ref, score_w, spread_w, stat_w, pick, stack):
     scores = []
     for x in xs:
         both = dot(x, score_w[...])
@@ -226,7 +282,7 @@
     rest = logsum - high.astype(F32)
     middle = rest.astype(BF)
     low = (rest - middle.astype(F32)).astype(BF)
-    stats = dot(jnp.concatenate([high, middle, low, meta_ref[...]], axis=1), stat_w[...])
+    stats = dot(jnp.concatenate([high, middle, low, meta], axis=1), stat_w[...])
     slot = iota((CHUNK, D), 0)
     rank = slot - PER * div(slot, float(PER))
     block = div(iota((CHUNK, D), 1), 64.0)
@@ -237,139 +293,170 @@
         stack[(3 + a) * CHUNK : (4 + a) * CHUNK, :] = jnp.where(
             block == k - 8.0 * div(k, 8.0), tiled, 0.0
         ).astype(BF)
-    out_ref[...] = dot(pick[...], stack[...]).astype(BF)
-
-
-def encode(own, got, meta, enc_kv, latent_query):
+    return dot(pick[...], stack[...]).astype(BF)
+
+
+def settle_tables(select, mask, fold):
+    m = iota((256, 256), 0)
+    k = m - MSG * div(m, float(MSG))
+    select[...] = hot((k < 27.0) & (iota((256, 256), 1) == m - k + 27.0 + div(k, 8.0)))
+    k = iota((256, D), 0)
+    k = k - MSG * div(k, float(MSG))
+    mask[...] = hot(div(iota((256, D), 1), 64.0) == k - 8.0 * div(k, 8.0))
+    lane = iota((D, D), 0)
+    lane = lane - 64.0 * div(lane, 64.0)
+    fold[:, 0:D] = hot((lane < 48.0) & (lane - 16.0 * div(lane, 16.0) == div(iota((D, D), 1), 32.0)))
+    lane = iota((D, 128), 0)
+    lane = lane - 64.0 * div(lane, 64.0)
+    fold[:, D : D + 128] = jnp.where(lane == 48.0, 16.0, jnp.where(lane == 49.0, 1.0, 0.0)).astype(BF)
+
+
+def settle_chunk(values, query_ref, out_w_ref, select, mask, fold):
+    stats = [(dot(select[...], v) * mask[...].astype(F32)).astype(BF) for v in values]
+    logs = [dot(s, fold[:, 0:D]) for s in stats]
+    peak = jnp.maximum(logs[0], logs[1])
+    weights = [jnp.exp(l - peak) for l in logs]
+    mixed = weights[0] * values[0].astype(F32) + weights[1] * values[1].astype(F32)
+    encoded = (mixed / (weights[0] + weights[1])).astype(BF)
+    q = query_ref[...].astype(F32)
+    k = iota((256, D), 0)
+    k = k - MSG * div(k, float(MSG))
+    bias = jnp.where(k < 9.0, q[0:1], jnp.where(k < 18.0, q[1:2], q[2:3]))
+    latents = (dot(encoded, out_w_ref[...]) + bias).astype(BF)
+    k = k[:, 0:128]
+    place = dot(stats[0], fold[:, D : D + 128]) + 6.0 * div(k, 9.0)
+    place = jnp.where(k < 27.0, place, FAR)
+    return latents, jnp.transpose(place)[0:8, :]
+
+
+def encode_kernel(
+    keep_ref,
+    got_ref,
+    meta_ref,
+    kv_ref,
+    query_ref,
+    out_w_ref,
+    grid_ref,
+    own,
+    mate,
+    score_w,
+    spread_w,
+    stat_w,
+    pick,
+    stack,
+    messages,
+    landed,
+    select,
+    mask,
+    fold,
+    latents,
+    rows,
+    load_sem,
+    send_sem,
+    recv_sem,
+):
+    barrier = pltpu.get_barrier_semaphore()
+
+    def load(i):
+        part = pl.ds(pl.multiple_of(i * CHUNK, 16), CHUNK)
+        return (
+            pltpu.make_async_copy(keep_ref.at[:, part], own.at[:, part], load_sem.at[2 * i]),
+            pltpu.make_async_copy(got_ref.at[:, part], mate.at[:, part], load_sem.at[2 * i + 1]),
+        )
+
+    for i in range(4):
+        for part in load(i):
+            part.start()
+
+    @pl.loop(1, 64)
+    def _(j):
+        pl.semaphore_signal(barrier, inc=1, device_id=receiver(j), device_id_type=MESH)
+
+    encode_tables(kv_ref, query_ref, score_w, spread_w, stat_w, pick)
+
+    def copy(j):
+        part = pl.ds(pl.multiple_of(j * MSG, MSG), MSG)
+        return pltpu.make_async_remote_copy(
+            src_ref=messages.at[part],
+            dst_ref=landed.at[part],
+            send_sem=send_sem.at[j],
+            recv_sem=recv_sem.at[j],
+            device_id=receiver(j),
+            device_id_type=MESH,
+        )
+
+    def sixteen(i, act):
+        @pl.loop(0, 16)
+        def _(t):
+            @pl.when(i * 16 + t > 0)
+            def _():
+                act(copy(i * 16 + t))
+
+    @pl.loop(0, 4)
+    def _(i):
+        for part in load(i):
+            part.wait()
+        part = pl.ds(pl.multiple_of(i * CHUNK, 16), CHUNK)
+        xs = [own[l, part, :] for l in range(3)] + [mate[l, part, :] for l in range(3)]
+        messages[pl.ds(pl.multiple_of(i * 512, 512), 512), :] = encode_chunk(
+            xs, meta_ref[part, :], kv_ref, score_w, spread_w, stat_w, pick, stack
+        )
+
+        @pl.when(i == 0)
+        def _():
+            landed[0:MSG, :] = messages[0:MSG, :]
+            pl.semaphore_wait(barrier, 63)
+
+        sixteen(i, lambda one: one.start())
+
+    settle_tables(select, mask, fold)
+
+    @pl.loop(0, 4)
+    def _(i):
+        sixteen(i, lambda one: one.wait())
+        values = [
+            landed[pl.ds(pl.multiple_of(i * 512 + g * 256, 256), 256), :] for g in range(2)
+        ]
+        done, place = settle_chunk(values, query_ref, out_w_ref, select, mask, fold)
+        part = pl.ds(pl.multiple_of(i * 256, 256), 256)
+        latents[part, :] = done
+        rows[:, part] = place
+
+    where = rows[0:1, :]
+    for b in range(4):
+        chosen = hot(iota((224, 1024), 0) + 224.0 * b == where)
+        grid_ref[b * 224 : (b + 1) * 224, :] = dot(chosen, latents[...]).astype(BF)
+
+
+def encode(keep, got, meta, enc_kv, latent_query, enc_out):
+    levels = pltpu.VMEM((3, 576, D), BF)
     return pl.pallas_call(
         encode_kernel,
-        grid=(576 // CHUNK,),
-        in_specs=[
-            pl.BlockSpec((3, CHUNK, D), lambda i: (0, i, 0)),
-            pl.BlockSpec((3, CHUNK, D), lambda i: (0, i, 0)),
-            pl.BlockSpec((CHUNK, 128), lambda i: (i, 0)),
-            VMEM,
-            VMEM,
-        ],
-        out_specs=pl.BlockSpec((16 * MSG, D), lambda i: (i, 0)),
-        out_shape=jax.ShapeDtypeStruct((64 * MSG, D), BF),
+        in_specs=[HBM, HBM] + [VMEM] * 4,
+        out_specs=VMEM,
+        out_shape=jax.ShapeDtypeStruct((896, D), BF),
         scratch_shapes=[
+            levels,
+            levels,
             pltpu.VMEM((D, 256), BF),
             pltpu.VMEM((128, LATENT * D), BF),
             pltpu.VMEM((512, LATENT * 128), BF),
             pltpu.VMEM((16 * MSG, 6 * CHUNK), BF),
             pltpu.VMEM((6 * CHUNK, D), BF),
-        ],
-        compiler_params=params(),
-        name="encode",
-    )(own, got, meta, enc_kv, latent_query)
-
-
-def swap_kernel(msg_ref, out_ref, send_sem, recv_sem, own_sem):
-    lev = lax.axis_index("lev")
-    win = lax.axis_index("win")
-    core = lax.rem(lev, 2)
-    me = (lev // 2) * N_WIN + win
-    count = 2 * N_WIN
-
-    def device(index):
-        return ((index // N_WIN) * 2 + core, lax.rem(index, N_WIN))
-
-    own = pltpu.make_async_copy(msg_ref.at[me], out_ref.at[me], own_sem)
-    own.start()
-    barrier = pltpu.get_barrier_semaphore()
-
-    @pl.loop(1, count)
-    def _(k):
-        pl.semaphore_signal(
-            barrier, inc=1, device_id=device(lax.rem(me + k, count)), device_id_type=MESH
-        )
-
-    pl.semaphore_wait(barrier, count - 1)
-
-    def copy(k):
-        dest = lax.rem(me + k, count)
-        return pltpu.make_async_remote_copy(
-            src_ref=msg_ref.at[dest],
-            dst_ref=out_ref.at[me],
-            send_sem=send_sem.at[k],
-            recv_sem=recv_sem.at[k],
-            device_id=device(dest),
-            device_id_type=MESH,
-        )
-
-    @pl.loop(1, count)
-    def _(k):
-        copy(k).start()
-
-    @pl.loop(1, count)
-    def _(k):
-        copy(k).wait()
-
-    own.wait()
-
-
-def swap(messages):
-    return pl.pallas_call(
-        swap_kernel,
-        out_shape=jax.ShapeDtypeStruct((64, MSG, D), BF),
-        in_specs=[ANY],
-        out_specs=ANY,
-        scratch_shapes=[
+            pltpu.VMEM((64 * MSG, D), BF),
+            pltpu.VMEM((64 * MSG, D), BF),
+            pltpu.VMEM((256, 256), BF),
+            pltpu.VMEM((256, D), BF),
+            pltpu.VMEM((D, D + 128), BF),
+            pltpu.VMEM((1024, D), BF),
+            pltpu.VMEM((8, 1024), F32),
+            pltpu.SemaphoreType.DMA((8,)),
             pltpu.SemaphoreType.DMA((64,)),
             pltpu.SemaphoreType.DMA((64,)),
-            pltpu.SemaphoreType.DMA,
         ],
-        compiler_params=pltpu.CompilerParams(collective_id=0, has_side_effects=True),
-        name="swap",
-    )(messages)
-
-
-def settle_kernel(got_ref, query_ref, out_w_ref, grid_ref, latents, rows):
-    m = iota((256, 256), 0)
-    k = m - MSG * div(m, float(MSG))
-    pick = hot((k < 27.0) & (iota((256, 256), 1) == m - k + 27.0 + div(k, 8.0)))
-    k = iota((256, D), 0)
-    k = k - MSG * div(k, float(MSG))
-    mask = div(iota((256, D), 1), 64.0) == k - 8.0 * div(k, 8.0)
-    lane = iota((D, D), 0)
-    lane = lane - 64.0 * div(lane, 64.0)
-    fold = hot((lane < 48.0) & (lane - 16.0 * div(lane, 16.0) == div(iota((D, D), 1), 32.0)))
-    lane = iota((D, 128), 0)
-    lane = lane - 64.0 * div(lane, 64.0)
-    base_w = jnp.where(lane == 48.0, 16.0, jnp.where(lane == 49.0, 1.0, 0.0)).astype(BF)
-    q = query_ref[...].astype(F32)
-    bias = jnp.where(k < 9.0, q[0:1], jnp.where(k < 18.0, q[1:2], q[2:3]))
-    k = iota((256, 128), 0)
-    k = k - MSG * div(k, float(MSG))
-    for c in range(4):
-        values = [got_ref[g, c * 256 : (c + 1) * 256, :] for g in range(2)]
-        stats = [jnp.where(mask, dot(pick, v), 0.0).astype(BF) for v in values]
-        logs = [dot(s, fold) for s in stats]
-        peak = jnp.maximum(logs[0], logs[1])
-        weights = [jnp.exp(l - peak) for l in logs]
-        mixed = weights[0] * values[0].astype(F32) + weights[1] * values[1].astype(F32)
-        encoded = (mixed / (weights[0] + weights[1])).astype(BF)
-        latents[c * 256 : (c + 1) * 256, :] = (dot(encoded, out_w_ref[...]) + bias).astype(BF)
-        place = dot(stats[0], base_w) + 6.0 * div(k, 9.0)
-        place = jnp.where(k < 27.0, place, FAR)
-        rows[:, c * 256 : (c + 1) * 256] = jnp.transpose(place)[0:8, :]
-    where = rows[0:1, :]
-    for b in range(4):
-        chosen = hot(iota((224, 1024), 0) + 224.0 * b == where)
-        grid_ref[b] = dot(chosen, latents[...]).astype(BF)
-
-
-def settle(got, latent_query, enc_out):
-    return pl.pallas_call(
-        settle_kernel,
-        in_specs=[VMEM] * 3,
-        out_specs=VMEM,
-        out_shape=jax.ShapeDtypeStruct((4, 224, D), BF),
-        scratch_shapes=[pltpu.VMEM((1024, D), BF), pltpu.VMEM((8, 1024), F32)],
-        compiler_params=params(),
-        name="settle",
-    )(got, latent_query, enc_out)
+        compiler_params=params(40, collective_id=0, has_side_effects=True),
+        name="encode",
+    )(keep, got, meta, enc_kv, latent_query, enc_out)
 
 
 def normalize(values):
@@ -633,7 +720,7 @@
         + [rows(896)] * 3
         + [pltpu.VMEM((224, D), F32), rows(224, 3 * D), rows(224), rows(224, 6 * D), rows(224, 2 * D)]
         + [pltpu.SemaphoreType.DMA((12,)), pltpu.SemaphoreType.DMA((12,)), pltpu.SemaphoreType.DMA((8,))],
-        compiler_params=params(collective_id=1, has_side_effects=True),
+        compiler_params=params(44, collective_id=1, has_side_effects=True),
         name="unet",
     )(shifts, grid, *tables(), *weights)
 
@@ -654,18 +741,10 @@
     qkv_c,
     proj_c,
 ):
-    lev_at = lax.axis_index("lev")
-    win_at = lax.axis_index("win")
-    slots = lax.dynamic_slice_in_dim(patch_order, win_at * PSH, PSH, 0).reshape(1, PSH)
-    core = lax.rem(lev_at, 2).astype(jnp.int32).reshape(1)
-    keep, send, meta = sort_fields(core, slots, fields)
-    got = lax.ppermute(send, "lev", [(0, 1), (1, 0), (2, 3), (3, 2)])
-    messages = encode(keep, got, meta, enc_kv, latent_query)
-    arrived = swap(messages.reshape(64, MSG, D)).reshape(2, 32 * MSG, D)
-    grid = settle(arrived, latent_query, enc_out)
-
+    keep, got, meta = sort_fields(patch_order.reshape(288, 128), fields)
+    grid = encode(keep, got, meta, enc_kv, latent_query, enc_out)
     weights = (qkv_a, proj_a, merge_w, qkv_b, proj_b, expand_w, qkv_c, proj_c)
-    result = unet(shift_offsets, grid.reshape(896, D), weights)
+    result = unet(shift_offsets, grid, weights)
     return result.reshape(PLAT, LATENT, PLON, D).transpose(0, 2, 1, 3)
 
 

time: 140 us -> 112 us (0.80)
  Pallas kernels: 131 us -> 107 us
  waiting for transfers between devices: 3.9 us -> 0 us
    pallas_call x4 -> x2, Pallas kernels: 72.6 us -> 55.1 us  [the longest x1 45.2 us: encode(): pl.pallas_call(encode_kernel, in_specs=[HBM, HBM] + [VMEM] * 4, out_specs...]
    pallas_call x1, Pallas kernels: 58 us -> 52.1 us  [unet(): pl.pallas_call(unet_kernel, in_specs=[SMEM] + [VMEM] * 6 + [ANY] * 8, out...]
    ppermute x1 -> x0, waiting for transfers between devices: 3.9 us -> none  [local(): got = lax.ppermute(send, 'lev', [(0, 1), (1, 0), (2, 3), (3, 2)])]
    unnamed x3 -> x35, local copies, waits for them, and re-layouts: 3.39 us -> 4.84 us
  transfers between devices with their start and end apart: 1 -> 0, of which waited for: 1 -> 0; matrix products, arithmetic and copies ran while one was open for 0% -> 0% of each run, Pallas kernels for 0% -> 0%
where the time goes in v2:
time: 112 us
  Pallas kernels  107 us (96%)
  local copies, waits for them, and re-layouts  4.84 us (4%)
    pallas_call x1, Pallas kernels, unet(): pl.pallas_call(unet_kernel, in_specs=[SMEM] + [VMEM] * 6 + [ANY] * 8, out...  52.1 us
    pallas_call x1, Pallas kernels, encode(): pl.pallas_call(encode_kernel, in_specs=[HBM, HBM] + [VMEM] * 4, out_specs...  45.2 us
    pallas_call x1, Pallas kernels, sort_fields(): pl.pallas_call(sort_kernel, in_specs=[VMEM, ANY], out_specs=[VMEM, ANY, V...  9.87 us
    unnamed x35, local copies, waits for them, and re-layouts  4.84 us

profile of v2, /device:TPU:0, one launch (start us, length us, event | category | flops | bytes accessed | tf_op | source)
XLA Modules:
  0.0 112.3 jit_solution(17794187955613260841)
XLA Ops:
  0.0 0.0 copy-start.10
  0.0 0.0 copy-start.11
  0.0 9.9 %sort_fields.1 = (bf16[3,576,512]{2,1,0:T(8,128)(2,1)}, bf16[3,576,512]{2,1,0:T(8,128)(2,1)}, bf16[576,128]{1,0:T(8,128)(2,1)}) custom-call(s32[288,128]{1,0:T(8,128)} %bitcast.5, bf16[3,1152,512]{2,1,0:T(8,128)(2,1)} %fields_ref.1), custom_call_target="tpu_custom_call" | custom-call | tf_op jit(solution)/shard_map/sort_fields/pallas_call | solution.py:210
  9.9 0.0 copy-done.8
  9.9 0.0 copy-done.5
  9.9 0.0 copy-done.15
  9.9 0.0 copy-start.1
  10.0 1.5 %copy-done.1 = bf16[3,576,512]{2,1,0:T(8,128)(2,1)S(1)} copy-done((bf16[3,576,512]{2,1,0:T(8,128)(2,1)S(1)}, bf16[3,576,512]{2,1,0:T(8,128)(2,1)}, u32[]{:S(2)}) %copy-start.1) | copy-done | bytes 1769496
  11.4 1.5 %copy-done.2 = bf16[3,576,512]{2,1,0:T(8,128)(2,1)S(1)} copy-done((bf16[3,576,512]{2,1,0:T(8,128)(2,1)S(1)}, bf16[3,576,512]{2,1,0:T(8,128)(2,1)}, u32[]{:S(2)}) %copy-start.2) | copy-done | bytes 1769496
  12.9 0.9 copy-done.12
  13.8 0.0 copy-start.13
  13.8 0.0 copy-start.14
  13.8 0.0 copy-start.16
  13.9 45.2 %encode.1.own_ref = bf16[896,512]{1,0:T(8,128)(2,1)S(1)} custom-call(bf16[3,576,512]{2,1,0:T(8,128)(2,1)S(1)} %copy-done.1, bf16[3,576,512]{2,1,0:T(8,128)(2,1)S(1)} %copy-done.2, bf16[576,128]{1,0:T(8,128)(2,1)S(1)} %copy-done.12, bf16[512,1024]{1,0:T(8,128)(2,1)S(1)} %copy-done.5, bf16[3,512]{1,0:T(4,128)(2,1)S(1)} %copy-done.15, ...), custom_call_target="tpu_custom_call" | custom-call | tf_op jit(solution)/shard_map/encode/pallas_call | solution.py:433
  59.1 0.0 copy-done.7
  59.1 0.0 copy-done.9
  59.1 0.0 copy-done.10
  59.1 0.0 copy-done.11
  59.2 0.0 copy-done
  59.2 0.0 copy-done.3
  59.2 0.0 copy-done.4
  59.2 0.0 copy-done.6
  59.2 52.1 %unet.1 = bf16[864,512]{1,0:T(8,128)(2,1)S(1)} custom-call(s32[2]{0:T(128)S(1)} %copy-done.16, bf16[896,512]{1,0:T(8,128)(2,1)S(1)} %encode.1.own_ref, f32[1,1344]{1,0:T(1,128)S(1)} %copy-done.14, f32[896,1]{1,0:T(8,128)S(1)} %copy-done.10, f32[8,1344]{1,0:T(8,128)S(1)} %copy-done.13, f32[896,1]{1,0:T(8,128)S(1)} %copy-done.9, f32[864,1]{1,0:T(8,128)S(1)} %copy-done.11, ...), custom_call_target="tpu_custom_call" | custom-call | tf_op jit(solution)/shard_map/unet/pallas_call | solution.py:713
  111.3 0.9 copy.21
  (14 shorter events, 0.0 us)
Async XLA Ops:
  0.0 9.9 %copy-start.8 = (bf16[512,512]{1,0:T(8,128)(2,1)S(1)}, bf16[512,512]{1,0:T(8,128)(2,1)}, u32[]{:S(2)}) copy-start(bf16[512,512]{1,0:T(8,128)(2,1)} %out_w_ref.1) | copy-start | bytes 1572868
  0.0 9.9 %copy-start.5 = (bf16[512,1024]{1,0:T(8,128)(2,1)S(1)}, bf16[512,1024]{1,0:T(8,128)(2,1)}, u32[]{:S(2)}) copy-start(bf16[512,1024]{1,0:T(8,128)(2,1)} %kv_ref.1) | copy-start | bytes 3145732
  0.0 9.9 %copy-start.15 = (bf16[3,512]{1,0:T(4,128)(2,1)S(1)}, bf16[3,512]{1,0:T(4,128)(2,1)}, u32[]{:S(2)}) copy-start(bf16[3,512]{1,0:T(4,128)(2,1)} %query_ref.1) | copy-start | bytes 9220
  0.0 59.1 %copy-start.7 = (bf16[512,512]{1,0:T(8,128)(2,1)S(1)}, bf16[512,512]{1,0:T(8,128)(2,1)}, u32[]{:S(2)}) copy-start(bf16[512,512]{1,0:T(8,128)(2,1)} %proj_c.1) | copy-start | bytes 1572868
  0.0 59.1 %copy-start.9 = (f32[896,1]{1,0:T(8,128)S(1)}, f32[896,1]{1,0:T(8,128)}, u32[]{:S(2)}) copy-start(f32[896,1]{1,0:T(8,128)} %constant.13.clone.sub_ref) | copy-start | bytes 10756
  0.0 59.1 %copy-start.10 = (f32[896,1]{1,0:T(8,128)S(1)}, f32[896,1]{1,0:T(8,128)}, u32[]{:S(2)}) copy-start(f32[896,1]{1,0:T(8,128)} %constant.11.clone.windows_ref) | copy-start | bytes 10756
  0.0 59.1 %copy-start.11 = (f32[864,1]{1,0:T(8,128)S(1)}, f32[864,1]{1,0:T(8,128)}, u32[]{:S(2)}) copy-start(f32[864,1]{1,0:T(8,128)} %constant.14.clone.final_ref) | copy-start | bytes 10372
  9.9 1.5 %copy-start.1 = (bf16[3,576,512]{2,1,0:T(8,128)(2,1)S(1)}, bf16[3,576,512]{2,1,0:T(8,128)(2,1)}, u32[]{:S(2)}) copy-start(bf16[3,576,512]{2,1,0:T(8,128)(2,1)} %get-tuple-element.8.keep_ref) | copy-start | bytes 5308420
  11.4 1.5 %copy-start.2 = (bf16[3,576,512]{2,1,0:T(8,128)(2,1)S(1)}, bf16[3,576,512]{2,1,0:T(8,128)(2,1)}, u32[]{:S(2)}) copy-start(bf16[3,576,512]{2,1,0:T(8,128)(2,1)} %get-tuple-element.9.got_ref) | copy-start | bytes 5308420
  12.9 0.9 copy-start.12
  13.8 45.3 %copy-start = (bf16[1024,1024]{1,0:T(8,128)(2,1)S(1)}, bf16[1024,1024]{1,0:T(8,128)(2,1)}, u32[]{:S(2)}) copy-start(bf16[1024,1024]{1,0:T(8,128)(2,1)} %proj_b.1) | copy-start | bytes 6291460
  13.8 45.3 %copy-start.3 = (bf16[512,1536]{1,0:T(8,128)(2,1)S(1)}, bf16[512,1536]{1,0:T(8,128)(2,1)}, u32[]{:S(2)}) copy-start(bf16[512,1536]{1,0:T(8,128)(2,1)} %qkv_a.1) | copy-start | bytes 4718596
  13.8 45.4 %copy-start.4 = (bf16[512,1536]{1,0:T(8,128)(2,1)S(1)}, bf16[512,1536]{1,0:T(8,128)(2,1)}, u32[]{:S(2)}) copy-start(bf16[512,1536]{1,0:T(8,128)(2,1)} %qkv_c.1) | copy-start | bytes 4718596
  13.8 45.4 %copy-start.6 = (bf16[512,512]{1,0:T(8,128)(2,1)S(1)}, bf16[512,512]{1,0:T(8,128)(2,1)}, u32[]{:S(2)}) copy-start(bf16[512,512]{1,0:T(8,128)(2,1)} %proj_a.1) | copy-start | bytes 1572868
  13.8 45.4 %copy-start.13 = (f32[8,1344]{1,0:T(8,128)S(1)}, f32[8,1344]{1,0:T(8,128)}, u32[]{:S(2)}) copy-start(f32[8,1344]{1,0:T(8,128)} %constant.12.clone.held_ref) | copy-start | bytes 129028
  13.8 45.4 %copy-start.14 = (f32[1,1344]{1,0:T(1,128)S(1)}, f32[1,1344]{1,0:T(1,128)}, u32[]{:S(2)}) copy-start(f32[1,1344]{1,0:T(1,128)} %constant.10.clone.spread_ref) | copy-start | bytes 16132
  13.8 45.4 %copy-start.16 = (s32[2]{0:T(128)S(1)}, s32[2]{0:T(128)}, u32[]{:S(2)}) copy-start(s32[2]{0:T(128)} %shift_ref.1) | copy-start | bytes 28

commit v3 on v2

--- a/solution.py
+++ b/solution.py
@@ -28,7 +28,6 @@
 VMEM = pl.BlockSpec(memory_space=pltpu.VMEM)
 SMEM = pl.BlockSpec(memory_space=pltpu.SMEM)
 ANY = pl.BlockSpec(memory_space=pl.ANY)
-HBM = pl.BlockSpec(memory_space=pltpu.HBM)
 
 
 def params(mib=60, **more):
@@ -137,21 +136,9 @@
     return block * 16.0 + 8.0 * jnp.abs(half - my_half) + pair - 8.0 * block
 
 
-def sort_kernel(
-    order_ref, fields_ref, keep_ref, got_ref, meta_ref, perm, fields, outgoing, load_sem, send_sem, recv_sem
-):
-    lev = lax.axis_index("lev")
+def sort_slots(order_ref, perm):
     win = lax.axis_index("win")
-    mate = (lev + 1 - 2 * lax.rem(lev, 2), win)
-    loads = [
-        pltpu.make_async_copy(fields_ref.at[l], fields.at[l], load_sem.at[l]) for l in range(3)
-    ]
-    for load in loads:
-        load.start()
-    barrier = pltpu.get_barrier_semaphore()
-    pl.semaphore_signal(barrier, inc=1, device_id=mate, device_id_type=MESH)
-
-    core = lax.rem(lev, 2).astype(F32)
+    core = lax.rem(lax.axis_index("lev"), 2).astype(F32)
     p = jnp.concatenate([order_ref[pl.ds(9 * win + r, 1), :] for r in range(9)], axis=1).astype(F32)
     row = div(p, 768.0)
     column = p - row * 768.0
@@ -173,24 +160,6 @@
     target = key * PER + jnp.concatenate(ranks, axis=1)
     for b in range(PSH // 128):
         perm[b * 128 : (b + 1) * 128, :] = hot(iota((128, PSH), 0) + b * 128.0 == target)
-    pl.semaphore_wait(barrier, 1)
-    copies = []
-    for l in range(3):
-        loads[l].wait()
-        outgoing[l] = dot(perm[576:, :], fields[l]).astype(BF)
-        copies.append(
-            pltpu.make_async_remote_copy(
-                src_ref=outgoing.at[l],
-                dst_ref=got_ref.at[l],
-                send_sem=send_sem.at[l],
-                recv_sem=recv_sem.at[l],
-                device_id=mate,
-                device_id_type=MESH,
-            )
-        )
-        copies[l].start()
-    for l in range(3):
-        keep_ref[l] = dot(perm[:576, :], fields[l]).astype(BF)
     j = div(column, 2.0)
     group = div(j, 3.0)
     i = div(row, 2.0)
@@ -199,34 +168,7 @@
     high = div(base, 16.0)
     low = base - 16.0 * high
     at = iota((128, PSH), 0)
-    meta = jnp.where(at == 48.0, high, jnp.where(at == 49.0, low, 0.0)).astype(BF)
-    meta_ref[...] = dot_nt(perm[0:576, :], meta).astype(BF)
-    for copy in copies:
-        copy.wait()
-
-
-def sort_fields(order, fields):
-    levels = pltpu.VMEM((3, 576, D), BF)
-    return pl.pallas_call(
-        sort_kernel,
-        in_specs=[VMEM, ANY],
-        out_specs=[VMEM, ANY, VMEM],
-        out_shape=[
-            jax.ShapeDtypeStruct((3, 576, D), BF),
-            jax.ShapeDtypeStruct((3, 576, D), BF),
-            jax.ShapeDtypeStruct((576, 128), BF),
-        ],
-        scratch_shapes=[
-            pltpu.VMEM((PSH, PSH), BF),
-            pltpu.VMEM((3, PSH, D), BF),
-            levels,
-            pltpu.SemaphoreType.DMA((3,)),
-            pltpu.SemaphoreType.DMA((3,)),
-            pltpu.SemaphoreType.DMA((3,)),
-        ],
-        compiler_params=params(60, collective_id=2, has_side_effects=True),
-        name="sort_fields",
-    )(order, fields)
+    return jnp.where(at == 48.0, high, jnp.where(at == 49.0, low, 0.0)).astype(BF)
 
 
 def encode_tables(kv_ref, query_ref, score_w, spread_w, stat_w, pick):
@@ -329,16 +271,22 @@
     return latents, jnp.transpose(place)[0:8, :]
 
 
-def encode_kernel(
-    keep_ref,
-    got_ref,
-    meta_ref,
+def level_partials(
+    order_ref,
+    fields_ref,
     kv_ref,
     query_ref,
     out_w_ref,
-    grid_ref,
+    grid,
+    links,
+    halo,
+    weight_loads,
+    perm,
+    fields,
+    outgoing,
     own,
     mate,
+    meta,
     score_w,
     spread_w,
     stat_w,
@@ -351,28 +299,53 @@
     fold,
     latents,
     rows,
-    load_sem,
+    level_load,
+    level_send,
+    level_recv,
     send_sem,
     recv_sem,
 ):
+    lev = lax.axis_index("lev")
+    other = (lev + 1 - 2 * lax.rem(lev, 2), lax.axis_index("win"))
+    loads = [
+        pltpu.make_async_copy(fields_ref.at[l], fields.at[l], level_load.at[l]) for l in range(3)
+    ]
+    for load in loads + weight_loads[:7]:
+        load.start()
     barrier = pltpu.get_barrier_semaphore()
-
-    def load(i):
-        part = pl.ds(pl.multiple_of(i * CHUNK, 16), CHUNK)
-        return (
-            pltpu.make_async_copy(keep_ref.at[:, part], own.at[:, part], load_sem.at[2 * i]),
-            pltpu.make_async_copy(got_ref.at[:, part], mate.at[:, part], load_sem.at[2 * i + 1]),
-        )
-
-    for i in range(4):
-        for part in load(i):
-            part.start()
+    pl.semaphore_signal(barrier, inc=1, device_id=other, device_id_type=MESH)
 
     @pl.loop(1, 64)
     def _(j):
         pl.semaphore_signal(barrier, inc=1, device_id=receiver(j), device_id_type=MESH)
 
+    places = sort_slots(order_ref, perm)
+    pl.semaphore_wait(barrier, 64)
+    copies = []
+    for l in range(3):
+        loads[l].wait()
+        outgoing[l] = dot(perm[576:, :], fields[l]).astype(BF)
+        copies.append(
+            pltpu.make_async_remote_copy(
+                src_ref=outgoing.at[l],
+                dst_ref=mate.at[l],
+                send_sem=level_send.at[l],
+                recv_sem=level_recv.at[l],
+                device_id=other,
+                device_id_type=MESH,
+            )
+        )
+        copies[l].start()
+    for l in range(3):
+        own[l] = dot(perm[:576, :], fields[l]).astype(BF)
+    for load in weight_loads[7:]:
+        load.start()
+    meta[...] = dot_nt(perm[0:576, :], places).astype(BF)
+    for load in weight_loads[:2]:
+        load.wait()
     encode_tables(kv_ref, query_ref, score_w, spread_w, stat_w, pick)
+    for one in copies:
+        one.wait()
 
     def copy(j):
         part = pl.ds(pl.multiple_of(j * MSG, MSG), MSG)
@@ -394,21 +367,14 @@
 
     @pl.loop(0, 4)
     def _(i):
-        for part in load(i):
-            part.wait()
         part = pl.ds(pl.multiple_of(i * CHUNK, 16), CHUNK)
         xs = [own[l, part, :] for l in range(3)] + [mate[l, part, :] for l in range(3)]
         messages[pl.ds(pl.multiple_of(i * 512, 512), 512), :] = encode_chunk(
-            xs, meta_ref[part, :], kv_ref, score_w, spread_w, stat_w, pick, stack
+            xs, meta[part, :], kv_ref, score_w, spread_w, stat_w, pick, stack
         )
-
-        @pl.when(i == 0)
-        def _():
-            landed[0:MSG, :] = messages[0:MSG, :]
-            pl.semaphore_wait(barrier, 63)
-
         sixteen(i, lambda one: one.start())
 
+    landed[0:MSG, :] = messages[0:MSG, :]
     settle_tables(select, mask, fold)
 
     @pl.loop(0, 4)
@@ -423,40 +389,41 @@
         rows[:, part] = place
 
     where = rows[0:1, :]
-    for b in range(4):
+    for n, b in enumerate((0, 3, 1, 2)):
         chosen = hot(iota((224, 1024), 0) + 224.0 * b == where)
-        grid_ref[b * 224 : (b + 1) * 224, :] = dot(chosen, latents[...]).astype(BF)
-
-
-def encode(keep, got, meta, enc_kv, latent_query, enc_out):
+        grid[b * 224 : (b + 1) * 224, :] = dot(chosen, latents[...]).astype(BF)
+        if n == 1:
+            for one in links.cells(0, grid, halo):
+                one.start()
+
+
+def partial_scratch():
     levels = pltpu.VMEM((3, 576, D), BF)
-    return pl.pallas_call(
-        encode_kernel,
-        in_specs=[HBM, HBM] + [VMEM] * 4,
-        out_specs=VMEM,
-        out_shape=jax.ShapeDtypeStruct((896, D), BF),
-        scratch_shapes=[
-            levels,
-            levels,
-            pltpu.VMEM((D, 256), BF),
-            pltpu.VMEM((128, LATENT * D), BF),
-            pltpu.VMEM((512, LATENT * 128), BF),
-            pltpu.VMEM((16 * MSG, 6 * CHUNK), BF),
-            pltpu.VMEM((6 * CHUNK, D), BF),
-            pltpu.VMEM((64 * MSG, D), BF),
-            pltpu.VMEM((64 * MSG, D), BF),
-            pltpu.VMEM((256, 256), BF),
-            pltpu.VMEM((256, D), BF),
-            pltpu.VMEM((D, D + 128), BF),
-            pltpu.VMEM((1024, D), BF),
-            pltpu.VMEM((8, 1024), F32),
-            pltpu.SemaphoreType.DMA((8,)),
-            pltpu.SemaphoreType.DMA((64,)),
-            pltpu.SemaphoreType.DMA((64,)),
-        ],
-        compiler_params=params(40, collective_id=0, has_side_effects=True),
-        name="encode",
-    )(keep, got, meta, enc_kv, latent_query, enc_out)
+    return [
+        pltpu.VMEM((PSH, PSH), BF),
+        pltpu.VMEM((3, PSH, D), BF),
+        levels,
+        levels,
+        levels,
+        pltpu.VMEM((576, 128), BF),
+        pltpu.VMEM((D, 256), BF),
+        pltpu.VMEM((128, LATENT * D), BF),
+        pltpu.VMEM((512, LATENT * 128), BF),
+        pltpu.VMEM((16 * MSG, 6 * CHUNK), BF),
+        pltpu.VMEM((6 * CHUNK, D), BF),
+        pltpu.VMEM((64 * MSG, D), BF),
+        pltpu.VMEM((64 * MSG, D), BF),
+        pltpu.VMEM((256, 256), BF),
+        pltpu.VMEM((256, D), BF),
+        pltpu.VMEM((D, D + 128), BF),
+        pltpu.VMEM((1024, D), BF),
+        pltpu.VMEM((8, 1024), F32),
+        pltpu.SemaphoreType.DMA((3,)),
+        pltpu.SemaphoreType.DMA((3,)),
+        pltpu.SemaphoreType.DMA((3,)),
+        pltpu.SemaphoreType.DMA((64,)),
+        pltpu.SemaphoreType.DMA((64,)),
+    ]
 
 
 def normalize(values):
@@ -506,12 +473,6 @@
             (lev, lax.rem(win + 1, N_WIN)),
         )
 
-    def greet(self):
-        barrier = pltpu.get_barrier_semaphore()
-        for side in self.sides:
-            pl.semaphore_signal(barrier, inc=1, device_id=side, device_id_type=MESH)
-        pl.semaphore_wait(barrier, 2)
-
     def copy(self, side, sem, source, target):
         return pltpu.make_async_remote_copy(
             src_ref=source,
@@ -589,72 +550,29 @@
     )
 
 
-def unet_kernel(
-    shift_ref,
-    own_ref,
-    spread_ref,
-    windows_ref,
-    held_ref,
-    sub_ref,
-    final_ref,
-    qkv_a,
-    proj_a,
-    merge_w,
-    qkv_b,
-    proj_b,
-    expand_w,
-    qkv_c,
-    proj_c,
-    out_ref,
-    qkv_a_v,
-    proj_a_v,
-    merge_v,
-    qkv_b_v,
-    proj_b_v,
-    expand_v,
-    qkv_c_v,
-    proj_c_v,
-    halo_a,
-    halo_c,
-    land_a,
-    land_c,
-    results,
-    joined,
-    first,
-    x,
-    qkv,
-    mixed,
-    qkv_wide,
-    mixed_wide,
-    send,
-    recv,
-    weight_sem,
-):
+def step_kernel(shift_ref, order_ref, query_ref, fields_ref, *refs):
+    early, late = refs[:7], refs[7:15]
+    out_ref = refs[15]
+    kv, out_w, spread_ref, windows_ref, held_ref, sub_ref, final_ref = refs[16:23]
+    qkv_a_v, proj_a_v, merge_v, qkv_b_v, proj_b_v, expand_v, qkv_c_v, proj_c_v = refs[23:31]
+    halo_a, halo_c, land_a, land_c, x, qkv, mixed, qkv_wide, mixed_wide, send, recv, load_sem, grid = refs[31:44]
+    encoder = refs[44:]
+    fields = encoder[1]
+    results, joined, first = (fields.at[l, pl.ds(0, 896)] for l in range(3))
     links = Links(send, recv)
-    links.greet()
-    for copy in links.cells(0, own_ref, halo_a):
-        copy.start()
-    pairs = [
-        (qkv_a, qkv_a_v),
-        (proj_a, proj_a_v),
-        (merge_w, merge_v),
-        (qkv_b, qkv_b_v),
-        (proj_b, proj_b_v),
-        (expand_w, expand_v),
-        (qkv_c, qkv_c_v),
-        (proj_c, proj_c_v),
+    loads = [
+        pltpu.make_async_copy(a, b, load_sem.at[n])
+        for n, (a, b) in enumerate(zip(early + late, refs[16:31]))
     ]
-    loads = [pltpu.make_async_copy(a, b, weight_sem.at[n]) for n, (a, b) in enumerate(pairs)]
-    for load in loads:
-        load.start()
-    loads[0].wait()
-    loads[1].wait()
+    level_partials(
+        order_ref, fields_ref, kv, query_ref, out_w, grid, links, halo_a, loads, *encoder
+    )
+    for load in loads[2:]:
+        load.wait()
     shift = shift_ref[0]
     shifted_windows(
-        links, 0, shift, own_ref, halo_a, results, land_a, spread_ref, windows_ref, qkv_a_v, proj_a_v, x, qkv, mixed
-    )
-    for load in loads[2:]:
-        load.wait()
+        links, 0, shift, grid, halo_a, results, land_a, spread_ref, windows_ref, qkv_a_v, proj_a_v, x, qkv, mixed
+    )
     for band in range(2):
         for copy in links.results(2, band, results, land_a):
             copy.wait()
@@ -708,21 +626,22 @@
         out_ref[rows, :] = gathered(final_ref[rows, :], ids, results, land_c).astype(BF)
 
 
-def unet(shifts, grid, weights):
+def step(shifts, order, latent_query, fields, held):
     rows = lambda count, width=D: pltpu.VMEM((count, width), BF)
     return pl.pallas_call(
-        unet_kernel,
-        in_specs=[SMEM] + [VMEM] * 6 + [ANY] * 8,
+        step_kernel,
+        in_specs=[SMEM, VMEM, VMEM] + [ANY] * (1 + len(held)),
         out_specs=VMEM,
         out_shape=jax.ShapeDtypeStruct((PLAT * LATENT * PLON, D), BF),
-        scratch_shapes=[pltpu.VMEM(w.shape, BF) for w in weights]
+        scratch_shapes=[pltpu.VMEM(w.shape, w.dtype) for w in held]
         + [rows(448)] * 4
-        + [rows(896)] * 3
         + [pltpu.VMEM((224, D), F32), rows(224, 3 * D), rows(224), rows(224, 6 * D), rows(224, 2 * D)]
-        + [pltpu.SemaphoreType.DMA((12,)), pltpu.SemaphoreType.DMA((12,)), pltpu.SemaphoreType.DMA((8,))],
-        compiler_params=params(44, collective_id=1, has_side_effects=True),
-        name="unet",
-    )(shifts, grid, *tables(), *weights)
+        + [pltpu.SemaphoreType.DMA((12,)), pltpu.SemaphoreType.DMA((12,)), pltpu.SemaphoreType.DMA((15,))]
+        + [rows(896)]
+        + partial_scratch(),
+        compiler_params=params(62, collective_id=0, has_side_effects=True),
+        name="step",
+    )(shifts, order, latent_query, fields, *held)
 
 
 def local(
@@ -741,10 +660,9 @@
     qkv_c,
     proj_c,
 ):
-    keep, got, meta = sort_fields(patch_order.reshape(288, 128), fields)
-    grid = encode(keep, got, meta, enc_kv, latent_query, enc_out)
-    weights = (qkv_a, proj_a, merge_w, qkv_b, proj_b, expand_w, qkv_c, proj_c)
-    result = unet(shift_offsets, grid, weights)
+    held = (enc_kv, enc_out) + tables()
+    held = held + (qkv_a, proj_a, merge_w, qkv_b, proj_b, expand_w, qkv_c, proj_c)
+    result = step(shift_offsets, patch_order.reshape(288, 128), latent_query, fields, held)
     return result.reshape(PLAT, LATENT, PLON, D).transpose(0, 2, 1, 3)
 
 

time: 112 us -> 107 us (0.955)
  local copies, waits for them, and re-layouts: 4.84 us -> 2.14 us
  Pallas kernels: 107 us -> 105 us
    unnamed x35 -> x1, local copies, waits for them, and re-layouts: 4.84 us -> 2.14 us
    pallas_call x3 -> x1, Pallas kernels: 107 us -> 105 us  [step(): pl.pallas_call(step_kernel, in_specs=[SMEM, VMEM, VMEM] + [ANY] * (1 + le...]
where the time goes in v3:
time: 107 us
  Pallas kernels  105 us (98%)
  local copies, waits for them, and re-layouts  2.14 us (2%)
    pallas_call x1, Pallas kernels, step(): pl.pallas_call(step_kernel, in_specs=[SMEM, VMEM, VMEM] + [ANY] * (1 + le...  105 us

profile of v3, /device:TPU:0, one launch (start us, length us, event | category | flops | bytes accessed | tf_op | source)
XLA Modules:
  0.0 107.1 jit_solution(12897710431130004289)
XLA Ops:
  0.0 104.9 %step.1 = bf16[864,512]{1,0:T(8,128)(2,1)} custom-call(s32[2]{0:T(128)} %shift_ref.1, s32[288,128]{1,0:T(8,128)} %bitcast.5, bf16[3,512]{1,0:T(4,128)(2,1)} %query_ref.1, bf16[3,1152,512]{2,1,0:T(8,128)(2,1)} %fields_ref.1, bf16[512,1024]{1,0:T(8,128)(2,1)} %refs_0_.1, bf16[512,512]{1,0:T(8,128)(2,1)} %refs_1_.1, f32[1,1344]{1,0:T(1,128)} %constant.10.clone.refs_2_, ...), custom_call_target="tpu_custom_call" | custom-call | tf_op jit(solution)/shard_map/step/pallas_call | solution.py:631
  104.9 2.1 %copy.21 = bf16[12,24,3,512]{3,1,2,0:T(8,128)(2,1)} copy(bf16[12,24,3,512]{3,1,2,0:T(8,128)(2,1)} %bitcast.4) | data formatting | bytes 1769472

commit v4 on v3

--- a/solution.py
+++ b/solution.py
@@ -110,14 +110,16 @@
     return lev // 2, win // 8, lax.rem(win // 4, 2), lax.rem(win, 4), lax.rem(lev, 2)
 
 
-def receiver(j):
-    half, x, low, y, core = place_of_me()
-    k = lax.rem(((j // 16) * 8 + lax.rem(j, 8)) * 11, 32)
-    half = lax.rem(half + lax.rem(j // 8, 2), 2)
-    x = lax.rem(x + k // 8, 4)
-    low = lax.rem(low + lax.rem(k // 4, 2), 2)
-    y = lax.rem(y + lax.rem(k, 4), 4)
-    return (half * 2 + core, x * 8 + low * 4 + y)
+class Receivers:
+    def __init__(self):
+        half, x, low, self.y, core = place_of_me()
+        self.levs = [lax.rem(half + z, 2) * 2 + core for z in range(2)]
+        xs = [lax.rem(x + d, 4) * 8 for d in range(4)]
+        lows = [lax.rem(low + d, 2) * 4 for d in range(2)]
+        self.bases = [xs[p % 4] + lows[p // 4] for p in range(8)]
+
+    def of(self, i, z, p):
+        return (self.levs[z], self.bases[p] + lax.rem(self.y + i + p, 4))
 
 
 def message_of(half, shard):
@@ -128,15 +130,12 @@
     y = y - 4.0 * low
     x = x - my_x + 4.0
     x = x - 4.0 * div(x, 4.0)
-    y = y - my_y + 4.0
-    y = y - 4.0 * div(y, 4.0)
-    pair = 3.0 * (8.0 * x + 4.0 * jnp.abs(low - my_low) + y)
-    pair = pair - 32.0 * div(pair, 32.0)
-    block = div(pair, 8.0)
-    return block * 16.0 + 8.0 * jnp.abs(half - my_half) + pair - 8.0 * block
-
-
-def sort_slots(order_ref, perm):
+    i = y - my_y - x + 8.0
+    i = i - 4.0 * div(i, 4.0)
+    return 16.0 * i + 8.0 * jnp.abs(half - my_half) + x + 4.0 * jnp.abs(low - my_low)
+
+
+def sort_slots(order_ref, perm, greetings):
     win = lax.axis_index("win")
     core = lax.rem(lax.axis_index("lev"), 2).astype(F32)
     p = jnp.concatenate([order_ref[pl.ds(9 * win + r, 1), :] for r in range(9)], axis=1).astype(F32)
@@ -160,6 +159,8 @@
     target = key * PER + jnp.concatenate(ranks, axis=1)
     for b in range(PSH // 128):
         perm[b * 128 : (b + 1) * 128, :] = hot(iota((128, PSH), 0) + b * 128.0 == target)
+        for greet in greetings[b * 7 : (b + 1) * 7]:
+            greet()
     j = div(column, 2.0)
     group = div(j, 3.0)
     i = div(row, 2.0)
@@ -314,12 +315,15 @@
         load.start()
     barrier = pltpu.get_barrier_semaphore()
     pl.semaphore_signal(barrier, inc=1, device_id=other, device_id_type=MESH)
-
-    @pl.loop(1, 64)
-    def _(j):
-        pl.semaphore_signal(barrier, inc=1, device_id=receiver(j), device_id_type=MESH)
-
-    places = sort_slots(order_ref, perm)
+    receivers = Receivers()
+
+    def greeting(i, z, p):
+        return lambda: pl.semaphore_signal(
+            barrier, inc=1, device_id=receivers.of(i, z, p), device_id_type=MESH
+        )
+
+    peers = [(i, z, p) for i in range(4) for z in range(2) for p in range(8)][1:]
+    places = sort_slots(order_ref, perm, [greeting(*peer) for peer in peers])
     pl.semaphore_wait(barrier, 64)
     copies = []
     for l in range(3):
@@ -347,23 +351,25 @@
     for one in copies:
         one.wait()
 
-    def copy(j):
+    def copy(i, z, p):
+        j = i * 16 + z * 8 + p
         part = pl.ds(pl.multiple_of(j * MSG, MSG), MSG)
         return pltpu.make_async_remote_copy(
             src_ref=messages.at[part],
             dst_ref=landed.at[part],
             send_sem=send_sem.at[j],
             recv_sem=recv_sem.at[j],
-            device_id=receiver(j),
+            device_id=receivers.of(i, z, p),
             device_id_type=MESH,
         )
 
     def sixteen(i, act):
-        @pl.loop(0, 16)
-        def _(t):
-            @pl.when(i * 16 + t > 0)
-            def _():
-                act(copy(i * 16 + t))
+        @pl.when(i > 0)
+        def _():
+            act(copy(i, 0, 0))
+
+        for t in range(1, 16):
+            act(copy(i, t // 8, t % 8))
 
     @pl.loop(0, 4)
     def _(i):
@@ -544,12 +550,6 @@
     return held_ref[0:1, :] + 36.0 * jnp.where(held_ref[1:2, :] > 0.5, near, far)
 
 
-def gathered(target, ids, results, land):
-    return dot(hot(target == ids[:, 0:896]), results[...]) + dot(
-        hot(target == ids[:, 896:1344]), land[...]
-    )
-
-
 def step_kernel(shift_ref, order_ref, query_ref, fields_ref, *refs):
     early, late = refs[:7], refs[7:15]
     out_ref = refs[15]
@@ -570,18 +570,21 @@
     for load in loads[2:]:
         load.wait()
     shift = shift_ref[0]
+    ids = held_ids(shift, held_ref)
     shifted_windows(
         links, 0, shift, grid, halo_a, results, land_a, spread_ref, windows_ref, qkv_a_v, proj_a_v, x, qkv, mixed
     )
+    for sub in range(4):
+        rows = slice(sub * 224, (sub + 1) * 224)
+        first[rows, :] = dot(hot(sub_ref[rows, :] == ids[:, 0:896]), results[...]).astype(BF)
     for band in range(2):
         for copy in links.results(2, band, results, land_a):
             copy.wait()
-
-    ids = held_ids(shift, held_ref)
     total = jnp.zeros((224, 1), F32)
     for sub in range(4):
         rows = slice(sub * 224, (sub + 1) * 224)
-        piece = gathered(sub_ref[rows, :], ids, results, land_a)
+        piece = dot(hot(sub_ref[rows, :] == ids[:, 896:1344]), land_a[...])
+        piece = piece + first[rows, :].astype(F32)
         first[rows, :] = piece.astype(BF)
         total = total + jnp.sum(piece, axis=1, keepdims=True)
     centre = total * (1.0 / (4 * D))
@@ -617,13 +620,17 @@
     shifted_windows(
         links, 6, shift, joined, halo_c, results, land_c, spread_ref, windows_ref, qkv_c_v, proj_c_v, x, qkv, mixed
     )
+    ids = held_ids(shift, held_ref)
+    for b in range(4):
+        rows = slice(b * 216, (b + 1) * 216)
+        out_ref[rows, :] = dot(hot(final_ref[rows, :] == ids[:, 0:896]), results[...]).astype(BF)
     for band in range(2):
         for copy in links.results(8, band, results, land_c):
             copy.wait()
-    ids = held_ids(shift, held_ref)
     for b in range(4):
         rows = slice(b * 216, (b + 1) * 216)
-        out_ref[rows, :] = gathered(final_ref[rows, :], ids, results, land_c).astype(BF)
+        piece = dot(hot(final_ref[rows, :] == ids[:, 896:1344]), land_c[...])
+        out_ref[rows, :] = (piece + out_ref[rows, :].astype(F32)).astype(BF)
 
 
 def step(shifts, order, latent_query, fields, held):

time: 107 us -> 101 us (0.944)
  Pallas kernels: 105 us -> 99.2 us
    pallas_call x1, Pallas kernels: 105 us -> 99.2 us  [step(): pl.pallas_call(step_kernel, in_specs=[SMEM, VMEM, VMEM] + [ANY] * (1 + le...]
where the time goes in v4:
time: 101 us
  Pallas kernels  99.2 us (98%)
  local copies, waits for them, and re-layouts  2.14 us (2%)
    pallas_call x1, Pallas kernels, step(): pl.pallas_call(step_kernel, in_specs=[SMEM, VMEM, VMEM] + [ANY] * (1 + le...  99.2 us
    unnamed x1, local copies, waits for them, and re-layouts  2.14 us

profile of v4, /device:TPU:0, one launch (start us, length us, event | category | flops | bytes accessed | tf_op | source)
XLA Modules:
  0.0 101.3 jit_solution(5244135691940531185)
XLA Ops:
  0.0 99.2 %step.1 = bf16[864,512]{1,0:T(8,128)(2,1)} custom-call(s32[2]{0:T(128)} %shift_ref.1, s32[288,128]{1,0:T(8,128)} %bitcast.5, bf16[3,512]{1,0:T(4,128)(2,1)} %query_ref.1, bf16[3,1152,512]{2,1,0:T(8,128)(2,1)} %fields_ref.1, bf16[512,1024]{1,0:T(8,128)(2,1)} %refs_0_.1, bf16[512,512]{1,0:T(8,128)(2,1)} %refs_1_.1, f32[1,1344]{1,0:T(1,128)} %constant.10.clone.refs_2_, ...), custom_call_target="tpu_custom_call" | custom-call | tf_op jit(solution)/shard_map/step/pallas_call | solution.py:638
  99.2 2.1 %copy.21 = bf16[12,24,3,512]{3,1,2,0:T(8,128)(2,1)} copy(bf16[12,24,3,512]{3,1,2,0:T(8,128)(2,1)} %bitcast.4) | data formatting | bytes 1769472

commit v5 on v4

--- a/solution.py
+++ b/solution.py
@@ -55,22 +55,22 @@
 
 
 def group_ids(first_column, spare=None):
-    ids = np.zeros((4, 56), np.float32)
+    ids = np.zeros((4, 28), np.float32)
     for sub in range(4):
-        for q in range(56):
-            p = min(q, 53)
-            column = first_column + 2 * (p // 18) + (sub & 1)
-            ids[sub, q] = column * 36 + (2 * (p % 6) + (sub >> 1)) * 3 + p % 18 // 6
+        for q in range(28):
+            p = min(q, 26)
+            column = first_column + 2 * (p // 9) + (sub & 1)
+            ids[sub, q] = column * 36 + (2 * (p % 3) + (sub >> 1)) * 3 + p % 9 // 3
     if spare is not None:
-        ids[:, 54:] = spare
+        ids[:, 27:] = spare
     return ids
 
 
-def half_ids(band, first_column, spare=None):
+def half_ids(first_column, spare=None):
     ids = np.zeros((112,), np.float32)
     for q in range(112):
         p = min(q, 107)
-        ids[q] = (first_column + p // 18) * 36 + (band * 6 + p % 6) * 3 + p % 18 // 6
+        ids[q] = (first_column + p // 18) * 36 + p % 6 * 3 + p % 18 // 6
     if spare is not None:
         ids[108:] = spare
     return ids
@@ -79,25 +79,21 @@
 def tables():
     groups = [group_ids(6 * g, FAR).reshape(-1) for g in range(-1, 5)]
     spread = np.concatenate(groups[1:5] + [groups[0], groups[5]])
-    windows = np.concatenate(
-        [np.concatenate([half_ids(b, 0), half_ids(b, 6)]) for _ in range(2) for b in range(2)]
+    window = np.concatenate([half_ids(0), half_ids(6)])
+    held = np.zeros((8, 672), np.float32)
+    held[0] = np.concatenate(
+        [half_ids(c, FAR) for c in (0, 6, 0, 6, 6 - PLON, PLON)]
     )
-    held = np.zeros((8, 1344), np.float32)
-    held[0] = np.concatenate(
-        [np.concatenate([half_ids(b, 0, FAR), half_ids(b, 6, FAR)]) for _ in range(2) for b in range(2)]
-        + [half_ids(b, 6 - PLON, FAR) for b in range(2)]
-        + [half_ids(b, PLON, FAR) for b in range(2)]
-    )
-    held[1, :448] = 1.0
+    held[1, :224] = 1.0
     by_sub = np.stack([group_ids(6 * g) for g in range(4)], axis=1).reshape(-1)
-    final = np.zeros((PLAT, LATENT, PLON), np.float32)
-    for r in range(PLAT):
+    final = np.zeros((6, LATENT, PLON), np.float32)
+    for r in range(6):
         for a in range(LATENT):
             for c in range(PLON):
                 final[r, a, c] = c * 36 + r * 3 + a
     return (
         jnp.asarray(spread[None]),
-        jnp.asarray(windows[:, None]),
+        jnp.asarray(window[:, None]),
         jnp.asarray(held),
         jnp.asarray(by_sub[:, None]),
         jnp.asarray(final.reshape(-1, 1)),
@@ -163,9 +159,11 @@
             greet()
     j = div(column, 2.0)
     group = div(j, 3.0)
+    upper = div(row, 6.0)
+    row = row - 6.0 * upper
     i = div(row, 2.0)
     sub = 2.0 * (row - 2.0 * i) + column - 2.0 * j
-    base = group * 224.0 + sub * 56.0 + (j - 3.0 * group) * 18.0 + i
+    base = upper * 448.0 + group * 112.0 + sub * 28.0 + (j - 3.0 * group) * 9.0 + i
     high = div(base, 16.0)
     low = base - 16.0 * high
     at = iota((128, PSH), 0)
@@ -267,7 +265,7 @@
     bias = jnp.where(k < 9.0, q[0:1], jnp.where(k < 18.0, q[1:2], q[2:3]))
     latents = (dot(encoded, out_w_ref[...]) + bias).astype(BF)
     k = k[:, 0:128]
-    place = dot(stats[0], fold[:, D : D + 128]) + 6.0 * div(k, 9.0)
+    place = dot(stats[0], fold[:, D : D + 128]) + 3.0 * div(k, 9.0)
     place = jnp.where(k < 27.0, place, FAR)
     return latents, jnp.transpose(place)[0:8, :]
 
@@ -395,11 +393,11 @@
         rows[:, part] = place
 
     where = rows[0:1, :]
-    for n, b in enumerate((0, 3, 1, 2)):
+    for b in range(4):
         chosen = hot(iota((224, 1024), 0) + 224.0 * b == where)
         grid[b * 224 : (b + 1) * 224, :] = dot(chosen, latents[...]).astype(BF)
-        if n == 1:
-            for one in links.cells(0, grid, halo):
+        if b % 2 == 1:
+            for one in links.cells(0, b // 2, grid, halo):
                 one.start()
 
 
@@ -489,31 +487,23 @@
             device_id_type=MESH,
         )
 
-    def cells(self, base, own, halo):
+    def pair(self, sem, band, source, to_previous, to_next, target):
+        rows = [pl.ds(pl.multiple_of(first, 16), 112) for first in (to_previous, to_next)]
+        before = pl.ds(pl.multiple_of(band * 224, 16), 112)
+        after = pl.ds(pl.multiple_of(band * 224 + 112, 16), 112)
         return (
-            self.copy(0, base, own.at[pl.ds(0, 224)], halo.at[pl.ds(224, 224)]),
-            self.copy(1, base + 1, own.at[pl.ds(672, 224)], halo.at[pl.ds(0, 224)]),
-        )
-
-    def results(self, base, band, results, land):
-        first = pl.multiple_of(448 + band * 224, 16)
-        return (
-            self.copy(
-                0,
-                base + 2 * band,
-                results.at[pl.ds(first, 112)],
-                land.at[pl.ds(pl.multiple_of(224 + band * 112, 16), 112)],
-            ),
-            self.copy(
-                1,
-                base + 2 * band + 1,
-                results.at[pl.ds(pl.multiple_of(first + 112, 16), 112)],
-                land.at[pl.ds(pl.multiple_of(band * 112, 16), 112)],
-            ),
-        )
-
-
-def shifted_windows(links, base, shift, own, halo, results, land, spread_ref, windows_ref, w_ref, proj_ref, x, qkv, mixed):
+            self.copy(0, sem + 2 * band, source.at[rows[0]], target.at[after]),
+            self.copy(1, sem + 2 * band + 1, source.at[rows[1]], target.at[before]),
+        )
+
+    def cells(self, sem, band, own, halo):
+        return self.pair(sem, band, own, band * 448, band * 448 + 336, halo)
+
+    def results(self, sem, band, results, land):
+        return self.pair(sem, band, results, band * 448 + 224, band * 448 + 336, land)
+
+
+def shifted_windows(links, base, shift, own, halo, results, land, spread_ref, window_ref, w_ref, proj_ref, x, qkv, mixed):
     near, far = shift_starts(shift)
     valid = valid_keys(112, 108)
 
@@ -521,27 +511,26 @@
     def _(step):
         band = step // 2
         outer = lax.rem((step + 1) // 2, 2)
-        rows = pl.ds(pl.multiple_of((outer * 2 + band) * 224, 224), 224)
-        target = windows_ref[rows, :] + 36.0 * jnp.where(outer == 0, near, far)
-        x[...] = dot(hot(target == spread_ref[:, 0:896]), own[...])
-
-        @pl.when(step == 1)
-        def _():
-            for copy in links.cells(base, own, halo):
-                copy.wait()
+        cells = pl.ds(pl.multiple_of(band * 448, 448), 448)
+        target = window_ref[...] + 36.0 * jnp.where(outer == 0, near, far)
+        x[...] = dot(hot(target == spread_ref[:, 0:448]), own[cells, :])
 
         @pl.when(outer == 1)
         def _():
-            x[...] += dot(hot(target == spread_ref[:, 896:1344]), halo[...])
+            for copy in links.cells(base, band, own, halo):
+                copy.wait()
+            part = pl.ds(pl.multiple_of(band * 224, 224), 224)
+            x[...] += dot(hot(target == spread_ref[:, 448:672]), halo[part, :])
 
         qkv[...] = dot(normalize(x[...]).astype(BF), w_ref[...]).astype(BF)
         for g in range(4):
             heads_of_group(qkv, mixed, g, D, valid)
+        rows = pl.ds(pl.multiple_of(band * 448 + outer * 224, 224), 224)
         results[rows, :] = (x[...] + dot(mixed[...], proj_ref[...])).astype(BF)
 
         @pl.when(outer == 1)
         def _():
-            for copy in links.results(base + 2, band, results, land):
+            for copy in links.results(base + 4, band, results, land):
                 copy.start()
 
 
@@ -555,8 +544,8 @@
     out_ref = refs[15]
     kv, out_w, spread_ref, windows_ref, held_ref, sub_ref, final_ref = refs[16:23]
     qkv_a_v, proj_a_v, merge_v, qkv_b_v, proj_b_v, expand_v, qkv_c_v, proj_c_v = refs[23:31]
-    halo_a, halo_c, land_a, land_c, x, qkv, mixed, qkv_wide, mixed_wide, send, recv, load_sem, grid = refs[31:44]
-    encoder = refs[44:]
+    halo_a, halo_c, land_a, land_c, x, qkv, mixed, qkv_wide, mixed_wide, wide, send, recv, load_sem, grid = refs[31:45]
+    encoder = refs[45:]
     fields = encoder[1]
     results, joined, first = (fields.at[l, pl.ds(0, 896)] for l in range(3))
     links = Links(send, recv)
@@ -574,19 +563,24 @@
     shifted_windows(
         links, 0, shift, grid, halo_a, results, land_a, spread_ref, windows_ref, qkv_a_v, proj_a_v, x, qkv, mixed
     )
-    for sub in range(4):
-        rows = slice(sub * 224, (sub + 1) * 224)
-        first[rows, :] = dot(hot(sub_ref[rows, :] == ids[:, 0:896]), results[...]).astype(BF)
     for band in range(2):
-        for copy in links.results(2, band, results, land_a):
+        own = dot(hot(sub_ref[...] == ids[:, 0:448]), results[band * 448 : (band + 1) * 448, :])
+        for sub in range(4):
+            first[sub * 224 + band * 112 : sub * 224 + (band + 1) * 112, :] = own[
+                sub * 112 : (sub + 1) * 112
+            ].astype(BF)
+    for band in range(2):
+        for copy in links.results(4, band, results, land_a):
             copy.wait()
+        got = dot(hot(sub_ref[...] == ids[:, 448:672]), land_a[band * 224 : (band + 1) * 224, :])
+        for sub in range(4):
+            rows = slice(sub * 224 + band * 112, sub * 224 + (band + 1) * 112)
+            first[rows, :] = (got[sub * 112 : (sub + 1) * 112] + first[rows, :].astype(F32)).astype(BF)
     total = jnp.zeros((224, 1), F32)
     for sub in range(4):
-        rows = slice(sub * 224, (sub + 1) * 224)
-        piece = dot(hot(sub_ref[rows, :] == ids[:, 896:1344]), land_a[...])
-        piece = piece + first[rows, :].astype(F32)
-        first[rows, :] = piece.astype(BF)
-        total = total + jnp.sum(piece, axis=1, keepdims=True)
+        total = total + jnp.sum(
+            first[sub * 224 : (sub + 1) * 224, :].astype(F32), axis=1, keepdims=True
+        )
     centre = total * (1.0 / (4 * D))
     spread = jnp.zeros((224, 1), F32)
     for sub in range(4):
@@ -599,7 +593,7 @@
         down = down + dot((offsets * scale).astype(BF), merge_v[sub * D : (sub + 1) * D, :])
     down = down.astype(BF).astype(F32)
     qkv_wide[...] = dot(normalize(down).astype(BF), qkv_b_v[...]).astype(BF)
-    valid = valid_keys(56, 54)
+    valid = valid_keys(28, 27)
 
     @pl.loop(0, 2)
     def _(step):
@@ -611,26 +605,30 @@
     for sub in range(4):
         grown = dot(normed, expand_v[:, sub * D : (sub + 1) * D])
         grown = grown + first[sub * 224 : (sub + 1) * 224, :].astype(F32)
-        for g in range(4):
-            joined[g * 224 + sub * 56 : g * 224 + (sub + 1) * 56, :] = grown[g * 56 : (g + 1) * 56, :].astype(BF)
-
-    for copy in links.cells(6, joined, halo_c):
-        copy.start()
+        for g in range(8):
+            wide[g * 112 + sub * 28 : g * 112 + (sub + 1) * 28, :] = grown[g * 28 : (g + 1) * 28, :]
+
+    for band in range(2):
+        rows = slice(band * 448, (band + 1) * 448)
+        joined[rows, :] = wide[rows, :].astype(BF)
+        for copy in links.cells(8, band, joined, halo_c):
+            copy.start()
     shift = shift_ref[1]
     shifted_windows(
-        links, 6, shift, joined, halo_c, results, land_c, spread_ref, windows_ref, qkv_c_v, proj_c_v, x, qkv, mixed
+        links, 8, shift, joined, halo_c, results, land_c, spread_ref, windows_ref, qkv_c_v, proj_c_v, x, qkv, mixed
     )
     ids = held_ids(shift, held_ref)
-    for b in range(4):
-        rows = slice(b * 216, (b + 1) * 216)
-        out_ref[rows, :] = dot(hot(final_ref[rows, :] == ids[:, 0:896]), results[...]).astype(BF)
     for band in range(2):
-        for copy in links.results(8, band, results, land_c):
+        rows = slice(band * 432, (band + 1) * 432)
+        out_ref[rows, :] = dot(
+            hot(final_ref[...] == ids[:, 0:448]), results[band * 448 : (band + 1) * 448, :]
+        ).astype(BF)
+    for band in range(2):
+        for copy in links.results(12, band, results, land_c):
             copy.wait()
-    for b in range(4):
-        rows = slice(b * 216, (b + 1) * 216)
-        piece = dot(hot(final_ref[rows, :] == ids[:, 896:1344]), land_c[...])
-        out_ref[rows, :] = (piece + out_ref[rows, :].astype(F32)).astype(BF)
+        rows = slice(band * 432, (band + 1) * 432)
+        got = dot(hot(final_ref[...] == ids[:, 448:672]), land_c[band * 224 : (band + 1) * 224, :])
+        out_ref[rows, :] = (got + out_ref[rows, :].astype(F32)).astype(BF)
 
 
 def step(shifts, order, latent_query, fields, held):
@@ -643,7 +641,8 @@
         scratch_shapes=[pltpu.VMEM(w.shape, w.dtype) for w in held]
         + [rows(448)] * 4
         + [pltpu.VMEM((224, D), F32), rows(224, 3 * D), rows(224), rows(224, 6 * D), rows(224, 2 * D)]
-        + [pltpu.SemaphoreType.DMA((12,)), pltpu.SemaphoreType.DMA((12,)), pltpu.SemaphoreType.DMA((15,))]
+        + [pltpu.VMEM((896, D), F32)]
+        + [pltpu.SemaphoreType.DMA((16,)), pltpu.SemaphoreType.DMA((16,)), pltpu.SemaphoreType.DMA((15,))]
         + [rows(896)]
         + partial_scratch(),
         compiler_params=params(62, collective_id=0, has_side_effects=True),

time: 101 us -> 98.3 us (0.973)
  Pallas kernels: 99.2 us -> 96 us
    pallas_call x1, Pallas kernels: 99.2 us -> 96 us  [step(): pl.pallas_call(step_kernel, in_specs=[SMEM, VMEM, VMEM] + [ANY] * (1 + le...]
where the time goes in v5:
time: 98.3 us; the launch traced here: 98.2 us
  Pallas kernels  96 us (98%)
  local copies, waits for them, and re-layouts  2.14 us (2%)
    pallas_call x1, Pallas kernels, step(): pl.pallas_call(step_kernel, in_specs=[SMEM, VMEM, VMEM] + [ANY] * (1 + le...  96 us
    unnamed x1, local copies, waits for them, and re-layouts  2.14 us

profile of v5, /device:TPU:0, one launch (start us, length us, event | category | flops | bytes accessed | tf_op | source)
XLA Modules:
  0.0 98.2 jit_solution(6640662500664948146)
XLA Ops:
  0.0 96.0 %step.1 = bf16[864,512]{1,0:T(8,128)(2,1)} custom-call(s32[2]{0:T(128)} %shift_ref.1, s32[288,128]{1,0:T(8,128)} %bitcast.5, bf16[3,512]{1,0:T(4,128)(2,1)} %query_ref.1, bf16[3,1152,512]{2,1,0:T(8,128)(2,1)} %fields_ref.1, bf16[512,1024]{1,0:T(8,128)(2,1)} %refs_0_.1, bf16[512,512]{1,0:T(8,128)(2,1)} %refs_1_.1, f32[1,672]{1,0:T(1,128)} %constant.10.clone.refs_2_, ...), custom_call_target="tpu_custom_call" | custom-call | tf_op jit(solution)/shard_map/step/pallas_call | solution.py:636
  96.0 2.1 %copy.21 = bf16[12,24,3,512]{3,1,2,0:T(8,128)(2,1)} copy(bf16[12,24,3,512]{3,1,2,0:T(8,128)(2,1)} %bitcast.4) | data formatting | bytes 1769472

commit v6 on v5

--- a/solution.py
+++ b/solution.py
@@ -340,8 +340,6 @@
         copies[l].start()
     for l in range(3):
         own[l] = dot(perm[:576, :], fields[l]).astype(BF)
-    for load in weight_loads[7:]:
-        load.start()
     meta[...] = dot_nt(perm[0:576, :], places).astype(BF)
     for load in weight_loads[:2]:
         load.wait()
@@ -367,7 +365,7 @@
             act(copy(i, 0, 0))
 
         for t in range(1, 16):
-            act(copy(i, t // 8, t % 8))
+            act(copy(i, t % 2, t // 2))
 
     @pl.loop(0, 4)
     def _(i):
@@ -378,6 +376,8 @@
         )
         sixteen(i, lambda one: one.start())
 
+    for load in weight_loads[7:]:
+        load.start()
     landed[0:MSG, :] = messages[0:MSG, :]
     settle_tables(select, mask, fold)
 

time: 98.3 us -> 97.5 us (level)
  no operation moved by 1% of the time
where the time goes in v6:
time: 97.5 us; the launch traced here: 97.3 us
  Pallas kernels  95.2 us (98%)
  local copies, waits for them, and re-layouts  2.14 us (2%)
    pallas_call x1, Pallas kernels, step(): pl.pallas_call(step_kernel, in_specs=[SMEM, VMEM, VMEM] + [ANY] * (1 + le...  95.2 us
    unnamed x1, local copies, waits for them, and re-layouts  2.14 us

profile of v6, /device:TPU:0, one launch (start us, length us, event | category | flops | bytes accessed | tf_op | source)
XLA Modules:
  0.0 97.3 jit_solution(8831332868927708729)
XLA Ops:
  0.0 95.2 %step.1 = bf16[864,512]{1,0:T(8,128)(2,1)} custom-call(s32[2]{0:T(128)} %shift_ref.1, s32[288,128]{1,0:T(8,128)} %bitcast.5, bf16[3,512]{1,0:T(4,128)(2,1)} %query_ref.1, bf16[3,1152,512]{2,1,0:T(8,128)(2,1)} %fields_ref.1, bf16[512,1024]{1,0:T(8,128)(2,1)} %refs_0_.1, bf16[512,512]{1,0:T(8,128)(2,1)} %refs_1_.1, f32[1,672]{1,0:T(1,128)} %constant.10.clone.refs_2_, ...), custom_call_target="tpu_custom_call" | custom-call | tf_op jit(solution)/shard_map/step/pallas_call | solution.py:636
  95.2 2.1 %copy.21 = bf16[12,24,3,512]{3,1,2,0:T(8,128)(2,1)} copy(bf16[12,24,3,512]{3,1,2,0:T(8,128)(2,1)} %bitcast.4) | data formatting | bytes 1769472

commit v7 on v6

--- a/solution.py
+++ b/solution.py
@@ -205,19 +205,20 @@
         pick[b * 128 : (b + 1) * 128, :] = hot(iota((128, 6 * CHUNK), 0) + b * 128.0 == row)
 
 
-def encode_chunk(xs, meta, kv_ref, score_w, spread_w, stat_w, pick, stack):
-    scores = []
-    for x in xs:
-        both = dot(x, score_w[...])
-        scores.append(both[:, :128] + both[:, 128:])
+def encode_chunk(x, meta, kv_ref, score_w, spread_w, stat_w, pick, stack):
+    parts = [slice(l * CHUNK, (l + 1) * CHUNK) for l in range(6)]
+    both = dot(x, score_w[...])
+    both = both[:, :128] + both[:, 128:]
+    scores = [both[part] for part in parts]
     peak = functools.reduce(jnp.maximum, scores)
     weights = [jnp.exp(s - peak) for s in scores]
     total = functools.reduce(jnp.add, weights)
-    mixes = [jnp.zeros((CHUNK, D), F32)] * LATENT
-    for x, w in zip(xs, weights):
-        value = dot(x, kv_ref[:, D:]).astype(BF).astype(F32)
-        wide = dot((w / total).astype(BF), spread_w[...])
-        mixes = [m + wide[:, a * D : (a + 1) * D] * value for a, m in enumerate(mixes)]
+    share = jnp.concatenate([(w / total).astype(BF) for w in weights], axis=0)
+    value = dot(x, kv_ref[:, D:]).astype(BF).astype(F32)
+    mixes = []
+    for a in range(LATENT):
+        mixed = dot(share, spread_w[:, a * D : (a + 1) * D]) * value
+        mixes.append(functools.reduce(jnp.add, [mixed[part] for part in parts]))
     logsum = peak + jnp.log(total)
     high = logsum.astype(BF)
     rest = logsum - high.astype(F32)
@@ -370,9 +371,9 @@
     @pl.loop(0, 4)
     def _(i):
         part = pl.ds(pl.multiple_of(i * CHUNK, 16), CHUNK)
-        xs = [own[l, part, :] for l in range(3)] + [mate[l, part, :] for l in range(3)]
+        x = jnp.concatenate([ref[l, part, :] for ref in (own, mate) for l in range(3)], axis=0)
         messages[pl.ds(pl.multiple_of(i * 512, 512), 512), :] = encode_chunk(
-            xs, meta[part, :], kv_ref, score_w, spread_w, stat_w, pick, stack
+            x, meta[part, :], kv_ref, score_w, spread_w, stat_w, pick, stack
         )
         sixteen(i, lambda one: one.start())
 
@@ -541,7 +542,8 @@
 
 def step_kernel(shift_ref, order_ref, query_ref, fields_ref, *refs):
     early, late = refs[:7], refs[7:15]
-    out_ref = refs[15]
+    own_ref, got_ref = refs[15:17]
+    refs = refs[1:]
     kv, out_w, spread_ref, windows_ref, held_ref, sub_ref, final_ref = refs[16:23]
     qkv_a_v, proj_a_v, merge_v, qkv_b_v, proj_b_v, expand_v, qkv_c_v, proj_c_v = refs[23:31]
     halo_a, halo_c, land_a, land_c, x, qkv, mixed, qkv_wide, mixed_wide, wide, send, recv, load_sem, grid = refs[31:45]
@@ -620,15 +622,16 @@
     ids = held_ids(shift, held_ref)
     for band in range(2):
         rows = slice(band * 432, (band + 1) * 432)
-        out_ref[rows, :] = dot(
+        own_ref[rows, :] = dot(
             hot(final_ref[...] == ids[:, 0:448]), results[band * 448 : (band + 1) * 448, :]
         ).astype(BF)
     for band in range(2):
         for copy in links.results(12, band, results, land_c):
             copy.wait()
         rows = slice(band * 432, (band + 1) * 432)
-        got = dot(hot(final_ref[...] == ids[:, 448:672]), land_c[band * 224 : (band + 1) * 224, :])
-        out_ref[rows, :] = (got + out_ref[rows, :].astype(F32)).astype(BF)
+        got_ref[rows, :] = dot(
+            hot(final_ref[...] == ids[:, 448:672]), land_c[band * 224 : (band + 1) * 224, :]
+        ).astype(BF)
 
 
 def step(shifts, order, latent_query, fields, held):
@@ -636,8 +639,8 @@
     return pl.pallas_call(
         step_kernel,
         in_specs=[SMEM, VMEM, VMEM] + [ANY] * (1 + len(held)),
-        out_specs=VMEM,
-        out_shape=jax.ShapeDtypeStruct((PLAT * LATENT * PLON, D), BF),
+        out_specs=[VMEM, VMEM],
+        out_shape=[jax.ShapeDtypeStruct((PLAT * LATENT * PLON, D), BF)] * 2,
         scratch_shapes=[pltpu.VMEM(w.shape, w.dtype) for w in held]
         + [rows(448)] * 4
         + [pltpu.VMEM((224, D), F32), rows(224, 3 * D), rows(224), rows(224, 6 * D), rows(224, 2 * D)]
@@ -668,7 +671,8 @@
 ):
     held = (enc_kv, enc_out) + tables()
     held = held + (qkv_a, proj_a, merge_w, qkv_b, proj_b, expand_w, qkv_c, proj_c)
-    result = step(shift_offsets, patch_order.reshape(288, 128), latent_query, fields, held)
+    own, got = step(shift_offsets, patch_order.reshape(288, 128), latent_query, fields, held)
+    result = own + got
     return result.reshape(PLAT, LATENT, PLON, D).transpose(0, 2, 1, 3)
 
 

time: 97.5 us -> 97.8 us (level)
  other arithmetic: 0 us -> 2.58 us
  local copies, waits for them, and re-layouts: 2.14 us -> 0 us
    add x0 -> x1, other arithmetic: none -> 2.58 us  [local(): result = own + got]
    unnamed x1 -> x0, local copies, waits for them, and re-layouts: 2.14 us -> none
where the time goes in v7:
time: 97.8 us; the launch traced here: 97.7 us
  Pallas kernels  95.1 us (97%)
  other arithmetic  2.58 us (3%)
    pallas_call x1, Pallas kernels, step(): pl.pallas_call(step_kernel, in_specs=[SMEM, VMEM, VMEM] + [ANY] * (1 + le...  95.1 us
    add x1, other arithmetic, local(): result = own + got  2.58 us

profile of v7, /device:TPU:0, one launch (start us, length us, event | category | flops | bytes accessed | tf_op | source)
XLA Modules:
  0.0 97.7 jit_solution(13314172907283834428)
XLA Ops:
  0.0 95.1 %step.1 = (bf16[864,512]{1,0:T(8,128)(2,1)}, bf16[864,512]{1,0:T(8,128)(2,1)}) custom-call(s32[2]{0:T(128)} %shift_ref.1, s32[288,128]{1,0:T(8,128)} %bitcast.4, bf16[3,512]{1,0:T(4,128)(2,1)} %query_ref.1, bf16[3,1152,512]{2,1,0:T(8,128)(2,1)} %fields_ref.1, bf16[512,1024]{1,0:T(8,128)(2,1)} %refs_0_.1, bf16[512,512]{1,0:T(8,128)(2,1)} %refs_1_.1, ...), custom_call_target="tpu_custom_call" | custom-call | tf_op jit(solution)/shard_map/step/pallas_call | solution.py:639
  95.1 2.6 %add.3 = bf16[864,512]{1,0:T(8,128)(2,1)} add(bf16[864,512]{1,0:T(8,128)(2,1)} %get-tuple-element.7, bf16[864,512]{1,0:T(8,128)(2,1)} %get-tuple-element.8) | non-fusion elementwise | flops 442368 | bytes 2654208 | tf_op jit(solution)/shard_map/add | solution.py:675

commit v8 on v7

--- a/solution.py
+++ b/solution.py
@@ -323,6 +323,10 @@
 
     peers = [(i, z, p) for i in range(4) for z in range(2) for p in range(8)][1:]
     places = sort_slots(order_ref, perm, [greeting(*peer) for peer in peers])
+    for load in weight_loads[:2]:
+        load.wait()
+    encode_tables(kv_ref, query_ref, score_w, spread_w, stat_w, pick)
+    settle_tables(select, mask, fold)
     pl.semaphore_wait(barrier, 64)
     copies = []
     for l in range(3):
@@ -342,9 +346,6 @@
     for l in range(3):
         own[l] = dot(perm[:576, :], fields[l]).astype(BF)
     meta[...] = dot_nt(perm[0:576, :], places).astype(BF)
-    for load in weight_loads[:2]:
-        load.wait()
-    encode_tables(kv_ref, query_ref, score_w, spread_w, stat_w, pick)
     for one in copies:
         one.wait()
 
@@ -380,7 +381,6 @@
     for load in weight_loads[7:]:
         load.start()
     landed[0:MSG, :] = messages[0:MSG, :]
-    settle_tables(select, mask, fold)
 
     @pl.loop(0, 4)
     def _(i):
@@ -542,8 +542,7 @@
 
 def step_kernel(shift_ref, order_ref, query_ref, fields_ref, *refs):
     early, late = refs[:7], refs[7:15]
-    own_ref, got_ref = refs[15:17]
-    refs = refs[1:]
+    out_ref = refs[15]
     kv, out_w, spread_ref, windows_ref, held_ref, sub_ref, final_ref = refs[16:23]
     qkv_a_v, proj_a_v, merge_v, qkv_b_v, proj_b_v, expand_v, qkv_c_v, proj_c_v = refs[23:31]
     halo_a, halo_c, land_a, land_c, x, qkv, mixed, qkv_wide, mixed_wide, wide, send, recv, load_sem, grid = refs[31:45]
@@ -622,16 +621,15 @@
     ids = held_ids(shift, held_ref)
     for band in range(2):
         rows = slice(band * 432, (band + 1) * 432)
-        own_ref[rows, :] = dot(
+        out_ref[rows, :] = dot(
             hot(final_ref[...] == ids[:, 0:448]), results[band * 448 : (band + 1) * 448, :]
         ).astype(BF)
     for band in range(2):
         for copy in links.results(12, band, results, land_c):
             copy.wait()
         rows = slice(band * 432, (band + 1) * 432)
-        got_ref[rows, :] = dot(
-            hot(final_ref[...] == ids[:, 448:672]), land_c[band * 224 : (band + 1) * 224, :]
-        ).astype(BF)
+        got = dot(hot(final_ref[...] == ids[:, 448:672]), land_c[band * 224 : (band + 1) * 224, :])
+        out_ref[rows, :] = (got + out_ref[rows, :].astype(F32)).astype(BF)
 
 
 def step(shifts, order, latent_query, fields, held):
@@ -639,8 +637,8 @@
     return pl.pallas_call(
         step_kernel,
         in_specs=[SMEM, VMEM, VMEM] + [ANY] * (1 + len(held)),
-        out_specs=[VMEM, VMEM],
-        out_shape=[jax.ShapeDtypeStruct((PLAT * LATENT * PLON, D), BF)] * 2,
+        out_specs=VMEM,
+        out_shape=jax.ShapeDtypeStruct((PLAT * LATENT * PLON, D), BF),
         scratch_shapes=[pltpu.VMEM(w.shape, w.dtype) for w in held]
         + [rows(448)] * 4
         + [pltpu.VMEM((224, D), F32), rows(224, 3 * D), rows(224), rows(224, 6 * D), rows(224, 2 * D)]
@@ -671,8 +669,7 @@
 ):
     held = (enc_kv, enc_out) + tables()
     held = held + (qkv_a, proj_a, merge_w, qkv_b, proj_b, expand_w, qkv_c, proj_c)
-    own, got = step(shift_offsets, patch_order.reshape(288, 128), latent_query, fields, held)
-    result = own + got
+    result = step(shift_offsets, patch_order.reshape(288, 128), latent_query, fields, held)
     return result.reshape(PLAT, LATENT, PLON, D).transpose(0, 2, 1, 3)
 
 

time: 97.8 us -> 96.3 us (0.985)
  other arithmetic: 2.58 us -> 0 us
  local copies, waits for them, and re-layouts: 0 us -> 2.14 us
  Pallas kernels: 95.1 us -> 94 us
    add x1 -> x0, other arithmetic: 2.58 us -> none  [local(): result = own + got]
    unnamed x0 -> x1, local copies, waits for them, and re-layouts: none -> 2.14 us
    pallas_call x1, Pallas kernels: 95.1 us -> 94 us  [step(): pl.pallas_call(step_kernel, in_specs=[SMEM, VMEM, VMEM] + [ANY] * (1 + le...]
where the time goes in v8:
time: 96.3 us; the launch traced here: 96.2 us
  Pallas kernels  94 us (98%)
  local copies, waits for them, and re-layouts  2.14 us (2%)
    pallas_call x1, Pallas kernels, step(): pl.pallas_call(step_kernel, in_specs=[SMEM, VMEM, VMEM] + [ANY] * (1 + le...  94 us
    unnamed x1, local copies, waits for them, and re-layouts  2.14 us

profile of v8, /device:TPU:0, one launch (start us, length us, event | category | flops | bytes accessed | tf_op | source)
XLA Modules:
  0.0 96.2 jit_solution(1124253860594070622)
XLA Ops:
  0.0 94.0 %step.1 = bf16[864,512]{1,0:T(8,128)(2,1)} custom-call(s32[2]{0:T(128)} %shift_ref.1, s32[288,128]{1,0:T(8,128)} %bitcast.5, bf16[3,512]{1,0:T(4,128)(2,1)} %query_ref.1, bf16[3,1152,512]{2,1,0:T(8,128)(2,1)} %fields_ref.1, bf16[512,1024]{1,0:T(8,128)(2,1)} %refs_0_.1, bf16[512,512]{1,0:T(8,128)(2,1)} %refs_1_.1, f32[1,672]{1,0:T(1,128)} %constant.10.clone.refs_2_, ...), custom_call_target="tpu_custom_call" | custom-call | tf_op jit(solution)/shard_map/step/pallas_call | solution.py:637
  94.0 2.1 %copy.21 = bf16[12,24,3,512]{3,1,2,0:T(8,128)(2,1)} copy(bf16[12,24,3,512]{3,1,2,0:T(8,128)(2,1)} %bitcast.4) | data formatting | bytes 1769472
